TPU v7x, 32 devices: a whole 2x2x4 slice. The times are simulated.
32 devices in a mesh: dp: 8 (over y, x, core), tensor: 4 (over z).
Axes of the slice: x: 2, y: 2, z: 4, core: 2. Of those that a mesh axis runs over, the one named last changes fastest.
Arguments:
- x_in: bfloat16 [16384, 1024], P(('dp', 'tensor')), may hold values from -6 to 6
- in_w: bfloat16 [1024, 3, 1024], P('dp', None, 'tensor'), may hold values from -0.1875 to 0.1875
- out_w: bfloat16 [1024, 1024], P('tensor', 'dp'), may hold values from -0.1875 to 0.1875
- gate_w: bfloat16 [1024, 4608], P('dp', 'tensor'), may hold values from -0.1875 to 0.1875
- up_w: bfloat16 [1024, 4608], P('dp', 'tensor'), may hold values from -0.1875 to 0.1875
- down_w: bfloat16 [4608, 1024], P('tensor', 'dp'), may hold values from -0.125 to 0.125
- conv_w: bfloat16 [3, 1024], replicated, may hold values from -3 to 3
- gain1: bfloat16 [1024], replicated, may hold values from 0.25 to 1.75
- gain2: bfloat16 [1024], replicated, may hold values from 0.25 to 1.75
- d_out: bfloat16 [16384, 1024], P(('dp', 'tensor')), may hold values from -6 to 6
Outputs:
- block_out: bfloat16 [16384, 1024], P(('dp', 'tensor'))
- d_x: bfloat16 [16384, 1024], P(('dp', 'tensor'))
- grad_in: float32 [1024, 3, 1024], P('dp', None, 'tensor')
- grad_out: float32 [1024, 1024], P('tensor', 'dp')
- grad_gate: float32 [1024, 4608], P('dp', 'tensor')
- grad_up: float32 [1024, 4608], P('dp', 'tensor')
- grad_down: float32 [4608, 1024], P('tensor', 'dp')
- grad_conv: float32 [3, 1024], replicated
- grad_gain1: float32 [1024], replicated
- grad_gain2: float32 [1024], replicated
All inputs are finite; a program needn't handle non-finite values.
Results may differ from a plain program's by a relative error of at most 0.018.
Values may be sent and summed in bfloat16 or wider, within the bound.
No kernel may reach another device: no remote copies, remote signals or barrier semaphores. Data moves between devices by JAX's collectives and lax.ppermute only.
A program may use at most 192 MiB of HBM per device.

v0:
```python
import jax
import jax.numpy as jnp
from jax import lax
from jax.sharding import PartitionSpec as P

LEN = 1024


epsilon = 1e-05


def in_blocks(x, dim, devices):
    before, after = (x.shape[:dim], x.shape[dim + 1 :])
    return jnp.moveaxis(x.reshape(*before, devices, -1, *after), dim, 0)


def sum_at_owner(x, axis, dim):
    tiles = in_blocks(x, dim, lax.axis_size(axis))
    arrived = lax.all_to_all(tiles, axis, split_axis=0, concat_axis=0, tiled=True)
    return arrived.astype(jnp.float32).sum(axis=0)


def norm_rows(values):
    scale = lax.rsqrt(jnp.mean(values * values, axis=-1, keepdims=True) + epsilon)
    return (values * scale, scale)


def norm_back(grad_h, normed, scale, gain):
    grad_n = grad_h * gain
    inner = jnp.mean(grad_n * normed, axis=-1, keepdims=True)
    return scale * (grad_n - normed * inner)


def delayed(values, steps_back):
    length = values.shape[1]
    padded = jnp.pad(values, ((0, 0), (steps_back, 0), (0, 0)))
    return padded[:, :length]


def advanced(values, steps_ahead):
    padded = jnp.pad(values, ((0, 0), (0, steps_ahead), (0, 0)))
    return padded[:, steps_ahead:]


def body(x_in, in_w, out_w, gate_w, up_w, down_w, conv_w, gain1, gain2, d_out):
    in_full, out_full, gate_full, up_full, down_full = (
        lax.all_gather(in_w, "dp", axis=0, tiled=True),
        lax.all_gather(out_w, "dp", axis=1, tiled=True),
        lax.all_gather(gate_w, "dp", axis=0, tiled=True),
        lax.all_gather(up_w, "dp", axis=0, tiled=True),
        lax.all_gather(down_w, "dp", axis=1, tiled=True),
    )
    model_width = x_in.shape[1]
    width = out_full.shape[0]
    offset = lax.axis_index("tensor") * width
    kernel = lax.dynamic_slice_in_dim(conv_w, offset, width, 1).astype(jnp.float32)
    gain_one = gain1.astype(jnp.float32)
    gain_two = gain2.astype(jnp.float32)
    tokens = x_in.astype(jnp.float32)
    normed_one, scale_one = norm_rows(tokens)
    first = (normed_one * gain_one).astype(jnp.bfloat16)
    first_all = lax.all_gather(first, "tensor", axis=0, tiled=True)
    group_rows = first_all.shape[0]
    seq_count = group_rows // LEN
    projected = jnp.einsum("td,dkc->tkc", first_all, in_full, preferred_element_type=jnp.float32)
    b_part = projected[:, 0].reshape(seq_count, LEN, width)
    c_part = projected[:, 1].reshape(seq_count, LEN, width)
    x_part = projected[:, 2].reshape(seq_count, LEN, width)
    mixed_in = b_part * x_part
    back_one = delayed(mixed_in, 1)
    back_two = delayed(mixed_in, 2)
    conv_out = kernel[2] * mixed_in + kernel[1] * back_one + kernel[0] * back_two
    branch = (c_part * conv_out).reshape(group_rows, width).astype(jnp.bfloat16)
    rows_now = branch
    mixed = lax.psum_scatter(
        jnp.dot(rows_now, out_full, preferred_element_type=jnp.float32).astype(jnp.bfloat16),
        "tensor",
        scatter_dimension=0,
        tiled=True,
    ).astype(jnp.float32)
    resid = tokens + mixed
    normed_two, scale_two = norm_rows(resid)
    second = (normed_two * gain_two).astype(jnp.bfloat16)
    second_all = lax.all_gather(second, "tensor", axis=0, tiled=True)
    gate = jnp.dot(second_all, gate_full, preferred_element_type=jnp.float32)
    up_val = jnp.dot(second_all, up_full, preferred_element_type=jnp.float32)
    sigma = jax.nn.sigmoid(gate)
    silu_gate = gate * sigma
    hidden = (silu_gate * up_val).astype(jnp.bfloat16)
    rows_now = hidden
    ffn = lax.psum_scatter(
        jnp.dot(rows_now, down_full, preferred_element_type=jnp.float32).astype(jnp.bfloat16),
        "tensor",
        scatter_dimension=0,
        tiled=True,
    ).astype(jnp.float32)
    block_out = (resid + ffn).astype(jnp.bfloat16)
    cot_all = lax.all_gather(d_out, "tensor", axis=0, tiled=True)
    d_hidden = jnp.einsum("td,fd->tf", cot_all, down_full, preferred_element_type=jnp.float32)
    d_gate = (d_hidden * up_val * sigma * (1.0 + gate * (1.0 - sigma))).astype(jnp.bfloat16)
    d_up = (d_hidden * silu_gate).astype(jnp.bfloat16)
    grad_down = jnp.einsum("tf,td->fd", hidden, cot_all, preferred_element_type=jnp.float32)
    grad_gate = jnp.einsum("td,tf->df", second_all, d_gate, preferred_element_type=jnp.float32)
    grad_up = jnp.einsum("td,tf->df", second_all, d_up, preferred_element_type=jnp.float32)
    grad_gate, grad_up, grad_down = (
        lax.psum_scatter(grad_gate, "dp", scatter_dimension=0, tiled=True),
        lax.psum_scatter(grad_up, "dp", scatter_dimension=0, tiled=True),
        lax.psum_scatter(grad_down, "dp", scatter_dimension=1, tiled=True),
    )
    part_gate = jnp.einsum("tf,df->td", d_gate, gate_full, preferred_element_type=jnp.float32)
    part_up = jnp.einsum("tf,df->td", d_up, up_full, preferred_element_type=jnp.float32)
    d_second = lax.psum_scatter(
        (part_gate + part_up).astype(jnp.bfloat16), "tensor", scatter_dimension=0, tiled=True
    ).astype(jnp.float32)
    gain_two_part = jnp.sum(d_second * normed_two, axis=0)
    d_resid = d_out.astype(jnp.float32) + norm_back(d_second, normed_two, scale_two, gain_two)
    d_mixed = lax.all_gather(d_resid.astype(jnp.bfloat16), "tensor", axis=0, tiled=True)
    grad_out = jnp.einsum("tc,td->cd", branch, d_mixed, preferred_element_type=jnp.float32)
    d_branch = jnp.einsum(
        "td,cd->tc", d_mixed, out_full, preferred_element_type=jnp.float32
    ).reshape(seq_count, LEN, width)
    d_conv = d_branch * c_part
    d_c = d_branch * conv_out
    d_mixin = kernel[2] * d_conv + kernel[1] * advanced(d_conv, 1) + kernel[0] * advanced(d_conv, 2)
    tap_two = jnp.sum(d_conv * mixed_in, axis=(0, 1))
    tap_one = jnp.sum(d_conv * back_one, axis=(0, 1))
    tap_zero = jnp.sum(d_conv * back_two, axis=(0, 1))
    d_b = d_mixin * x_part
    d_xpart = d_mixin * b_part
    d_proj = (
        jnp.stack([d_b, d_c, d_xpart], axis=2).reshape(group_rows, 3, width).astype(jnp.bfloat16)
    )
    grad_in = jnp.einsum("td,tkc->dkc", first_all, d_proj, preferred_element_type=jnp.float32)
    grad_in, grad_out = (
        sum_at_owner(grad_in.astype(jnp.bfloat16), "dp", 0),
        sum_at_owner(grad_out.astype(jnp.bfloat16), "dp", 1),
    )
    rows_now = d_proj
    d_first = lax.psum_scatter(
        jnp.einsum("tkc,dkc->td", rows_now, in_full, preferred_element_type=jnp.float32).astype(
            jnp.bfloat16
        ),
        "tensor",
        scatter_dimension=0,
        tiled=True,
    ).astype(jnp.float32)
    gain_one_part = jnp.sum(d_first * normed_one, axis=0)
    d_x = (d_resid + norm_back(d_first, normed_one, scale_one, gain_one)).astype(jnp.bfloat16)
    taps_local = jnp.stack([tap_zero, tap_one, tap_two], axis=0)
    taps_whole = lax.dynamic_update_slice_in_dim(
        jnp.zeros((3, model_width), jnp.float32), taps_local, offset, 1
    )
    grad_gain1, grad_gain2, grad_conv = lax.psum(
        (gain_one_part, gain_two_part, taps_whole), ("dp", "tensor")
    )
    return (
        block_out,
        d_x,
        grad_in,
        grad_out,
        grad_gate,
        grad_up,
        grad_down,
        grad_conv,
        grad_gain1,
        grad_gain2,
    )


def solution(mesh):
    in_specs = (
        P(("dp", "tensor"), None),
        P("dp", None, "tensor"),
        P("tensor", "dp"),
        P("dp", "tensor"),
        P("dp", "tensor"),
        P("tensor", "dp"),
        P(),
        P(),
        P(),
        P(("dp", "tensor"), None),
    )
    out_specs = (
        P(("dp", "tensor"), None),
        P(("dp", "tensor"), None),
        P("dp", None, "tensor"),
        P("tensor", "dp"),
        P("dp", "tensor"),
        P("dp", "tensor"),
        P("tensor", "dp"),
        P(),
        P(),
        P(),
    )
    return jax.shard_map(body, mesh=mesh, in_specs=in_specs, out_specs=out_specs, check_vma=False)
```

profile of v0, /device:TPU:0, one launch (start us, length us, event | category | flops | bytes accessed | tf_op | source)
XLA Modules:
  0.0 1019.6 jit_solution(11951078540977682232)
XLA Ops:
  13.5 12.6 %all_gather.29 = bf16[256,1024]{1,0:T(8,128)(2,1)S(1)} all-gather(bf16[256,128]{1,0:T(8,128)(2,1)S(1)} %copy-done.21), channel_id=1, replica_groups=mesh['dp'=8,'tensor'=4] {'dp'}, dimensions={1}, use_global_device_ids=true | all-gather | bytes 589824 | tf_op jit(solution)/shard_map/all_gather | solution.py:48
  26.1 12.9 %all-gather.11.cloned.1.call-done = bf16[1024,3,256]{2,0,1:T(8,128)(2,1)} async-done(((bf16[128,3,256]{2,0,1:T(8,128)(2,1)}), bf16[1024,3,256]{2,0,1:T(8,128)(2,1)}) %all-gather.11.cloned.1.call-update) | async-done | bytes 1572880 | tf_op jit(solution)/shard_map/all_gather | solution.py:47
  39.0 82.9 %all-gather.9.cloned.1.call-done = bf16[2048,1024]{1,0:T(8,128)(2,1)} async-done(((bf16[512,1024]{1,0:T(8,128)(2,1)}), bf16[2048,1024]{1,0:T(8,128)(2,1)}) %all-gather.9.cloned.1.call-update) | async-done | bytes 4194320 | tf_op jit(solution)/shard_map/all_gather | solution.py:62
  140.1 74.8 %reduce-scatter.8.cloned.1.call-done = bf16[512,1024]{1,0:T(8,128)(2,1)} async-done(((bf16[2048,1024]{1,0:T(8,128)(2,1)}), bf16[512,1024]{1,0:T(8,128)(2,1)}) %reduce-scatter.8.cloned.1.call-update) | async-done | bytes 1048592 | tf_op jit(solution)/shard_map/reduce_scatter | solution.py:75
  220.3 26.0 %all-gather.15.cloned.1.call-done = bf16[1024,1152]{1,0:T(8,128)(2,1)} async-done(((bf16[128,1152]{1,0:T(8,128)(2,1)}), bf16[1024,1152]{1,0:T(8,128)(2,1)}) %all-gather.15.cloned.1.call-update) | async-done | bytes 2359312 | tf_op jit(solution)/shard_map/all_gather | solution.py:49
  246.3 82.9 %all-gather.13.cloned.1.call-done = bf16[2048,1024]{1,0:T(8,128)(2,1)} async-done(((bf16[512,1024]{1,0:T(8,128)(2,1)}), bf16[2048,1024]{1,0:T(8,128)(2,1)}) %all-gather.13.cloned.1.call-update) | async-done | bytes 4194320 | tf_op jit(solution)/shard_map/all_gather | solution.py:84
  329.2 10.3 %fusion.39 = f32[2048,1152]{1,0:T(8,128)} fusion(bf16[2048,1024]{1,0:T(8,128)(2,1)} %all-gather.13.cloned.1.call-done, bf16[1024,1152]{1,0:T(8,128)(2,1)} %all-gather.15.cloned.1.call-done), kind=kOutput, calls=%fused_computation.77 | convolution fusion | flops 4831838208 | bytes 15990784 | tf_op jit(solution)/shard_map/dot_general | solution.py:85
  339.5 19.2 %all-gather.17.cloned.1.call-done = bf16[1024,1152]{1,0:T(8,128)(2,1)} async-done(((bf16[128,1152]{1,0:T(8,128)(2,1)}), bf16[1024,1152]{1,0:T(8,128)(2,1)}) %all-gather.17.cloned.1.call-update) | async-done | bytes 2359312 | tf_op jit(solution)/shard_map/all_gather | solution.py:50
  358.6 10.3 %fusion.40 = f32[2048,1152]{1,0:T(8,128)} fusion(bf16[2048,1024]{1,0:T(8,128)(2,1)} %all-gather.13.cloned.1.call-done, bf16[1024,1152]{1,0:T(8,128)(2,1)} %all-gather.17.cloned.1.call-done), kind=kOutput, calls=%fused_computation.78 | convolution fusion | flops 4831838208 | bytes 15990784 | tf_op jit(solution)/shard_map/dot_general | solution.py:86
  368.9 21.1 %all-gather.19.cloned.1.call-done = bf16[1152,1024]{1,0:T(8,128)(2,1)} async-done(((bf16[1152,128]{1,0:T(8,128)(2,1)}), bf16[1152,1024]{1,0:T(8,128)(2,1)}) %all-gather.19.cloned.1.call-update) | async-done | bytes 2359312 | tf_op jit(solution)/shard_map/all_gather | solution.py:51
  390.1 82.4 %all-gather.21.cloned.1.call-done = bf16[2048,1024]{1,0:T(8,128)(2,1)} async-done(((bf16[512,1024]{1,0:T(8,128)(2,1)}), bf16[2048,1024]{1,0:T(8,128)(2,1)}) %all-gather.21.cloned.1.call-update) | async-done | bytes 4194320 | tf_op jit(solution)/shard_map/all_gather | solution.py:98
  472.5 17.8 %multiply_convert_fusion = (bf16[2048,1152]{1,0:T(8,128)(2,1)}, bf16[2048,1152]{1,0:T(8,128)(2,1)}, bf16[2048,1152]{1,0:T(8,128)(2,1)}) fusion(f32[2048,1152]{1,0:T(8,128)} %fusion.39, f32[2048,1152]{1,0:T(8,128)} %fusion.40, bf16[2048,1024]{1,0:T(8,128)(2,1)} %all-gather.21.cloned.1.call-done, bf16[1152,1024]{1,0:T(8,128)(2,1)} %all-gather.19.cloned.1.call-done), kind=kOutput, calls=%fused_computation | convolution fusion | flops 4867227648 | bytes 39583744 | tf_op jit(solution)/shard_map/td,fd->tf/dot_general | solution.py:99
  505.9 75.4 %reduce-scatter.12.cloned.1.call-done = bf16[512,1024]{1,0:T(8,128)(2,1)} async-done(((bf16[2048,1024]{1,0:T(8,128)(2,1)}), bf16[512,1024]{1,0:T(8,128)(2,1)}) %reduce-scatter.12.cloned.1.call-update) | async-done | bytes 1048592 | tf_op jit(solution)/shard_map/reduce_scatter | solution.py:112
  585.4 81.4 %all-gather.23.cloned.1.call-done = bf16[2048,1024]{1,0:T(8,128)(2,1)} async-done(((bf16[512,1024]{1,0:T(8,128)(2,1)}), bf16[2048,1024]{1,0:T(8,128)(2,1)}) %all-gather.23.cloned.1.call-update) | async-done | bytes 4194320 | tf_op jit(solution)/shard_map/all_gather | solution.py:117
  682.6 9.5 convolution_convert_fusion
  692.1 10.7 %fusion.42 = f32[1024,1152]{1,0:T(8,128)} fusion(bf16[2048,1024]{1,0:T(8,128)(2,1)} %all-gather.13.cloned.1.call-done, bf16[2048,1152]{1,0:T(8,128)(2,1)} %get-tuple-element.25), kind=kOutput, calls=%fused_computation.80 | convolution fusion | flops 4831838208 | bytes 13631488 | tf_op jit(solution)/shard_map/td,tf->df/dot_general | solution.py:103
  702.9 10.3 %fusion.43 = f32[1024,1152]{1,0:T(8,128)} fusion(bf16[2048,1024]{1,0:T(8,128)(2,1)} %all-gather.13.cloned.1.call-done, bf16[2048,1152]{1,0:T(8,128)(2,1)} %get-tuple-element.24), kind=kOutput, calls=%fused_computation.81 | convolution fusion | flops 4831838208 | bytes 13631488 | tf_op jit(solution)/shard_map/td,tf->df/dot_general | solution.py:104
  713.3 9.8 fusion.44
  748.0 19.2 %all-to-all-done = bf16[8,128,3,256]{3,1,2,0:T(8,128)(2,1)} async-done(((bf16[8,128,3,256]{3,1,2,0:T(8,128)(2,1)}), bf16[8,128,3,256]{3,1,2,0:T(8,128)(2,1)}, u32[]{:S(2)}, u32[]{:S(2)}) %all-to-all-start) | async-done | bytes 1572896 | tf_op jit(solution)/shard_map/all_to_all | solution.py:19
  771.7 42.6 %all-reduce.4 = (f32[3,1024]{1,0:T(4,128)}, f32[1024]{0:T(1024)}, f32[1024]{0:T(1024)}) all-reduce(f32[3,1024]{1,0:T(4,128)S(1)} %maximum_dynamic-update-slice_fusion, f32[1024]{0:T(1024)S(1)} %get-tuple-element.14, f32[1024]{0:T(1024)S(1)} %get-tuple-element.12), channel_id=1, replica_groups=mesh['dp'=8,'tensor'=4] {'dp','tensor'}, use_global_device_ids=true, to_apply=%region_16.17 | all-reduce | flops 5120 | bytes 40960 | tf_op jit(solution)/shard_map/psum | solution.py:153
  814.3 24.2 %reduce-scatter.10.cloned.1.call-done = bf16[512,1024]{1,0:T(8,128)(2,1)} async-done(((bf16[2048,1024]{1,0:T(8,128)(2,1)}), bf16[512,1024]{1,0:T(8,128)(2,1)}) %reduce-scatter.10.cloned.1.call-update) | async-done | bytes 1048592 | tf_op jit(solution)/shard_map/reduce_scatter | solution.py:91
  842.7 54.2 %reduce-scatter.16.cloned.1.call-done = f32[128,1152]{1,0:T(8,128)} async-done(((f32[1024,1152]{1,0:T(8,128)}), f32[128,1152]{1,0:T(8,128)}) %reduce-scatter.16.cloned.1.call-update) | async-done | bytes 589840 | tf_op jit(solution)/shard_map/reduce_scatter | solution.py:106
  896.9 58.2 %reduce-scatter.18.cloned.1.call-done = f32[128,1152]{1,0:T(8,128)} async-done(((f32[1024,1152]{1,0:T(8,128)}), f32[128,1152]{1,0:T(8,128)}) %reduce-scatter.18.cloned.1.call-update) | async-done | bytes 589840 | tf_op jit(solution)/shard_map/reduce_scatter | solution.py:107
  955.1 57.8 %reduce-scatter.20.cloned.1.call-done = f32[1152,128]{1,0:T(8,128)} async-done(((f32[1152,1024]{1,0:T(8,128)}), f32[1152,128]{1,0:T(8,128)}) %reduce-scatter.20.cloned.1.call-update) | async-done | bytes 589840 | tf_op jit(solution)/shard_map/reduce_scatter | solution.py:108
  (128 shorter events, 98.7 us)
Async XLA Ops:
  7.2 31.9 %all-gather.11.cloned.1.call-start = ((), (), s32[]{:S(2)}) async-start(), calls=%async_computation.10 | async-start | bytes 1769472 | tf_op jit(solution)/shard_map/all_gather | solution.py:47
  7.9 114.1 %all-gather.9.cloned.1.call-start = ((), (), s32[]{:S(2)}) async-start(), calls=%async_computation.9 | async-start | bytes 5242880 | tf_op jit(solution)/shard_map/all_gather | solution.py:62
  10.2 111.8 %copy-start.22 = (f32[512]{0:T(512)}, f32[512]{0:T(512)S(1)}, u32[]{:S(2)}) copy-start(f32[512]{0:T(512)S(1)} %add_rsqrt_fusion.1) | copy-start | bytes 6148
  12.7 202.1 %reduce-scatter.8.cloned.1.call-start = ((), (), s32[]{:S(2)}) async-start(), calls=%async_computation.11 | async-start | bytes 5242880 | tf_op jit(solution)/shard_map/reduce_scatter | solution.py:75
  26.1 108.9 %copy-start.15 = (bf16[256,1024]{1,0:T(8,128)(2,1)}, bf16[256,1024]{1,0:T(8,128)(2,1)S(1)}, u32[]{:S(2)}) copy-start(bf16[256,1024]{1,0:T(8,128)(2,1)S(1)} %all_gather.29) | copy-start | bytes 1572868
  139.4 75.5 %copy-start = (bf16[512,1024]{1,0:T(8,128)(2,1)S(1)}, bf16[512,1024]{1,0:T(8,128)(2,1)}, u32[]{:S(2)}) copy-start(bf16[512,1024]{1,0:T(8,128)(2,1)} %param.10) | copy-start | bytes 3145732
  139.4 106.9 %all-gather.15.cloned.1.call-start = ((), (), s32[]{:S(2)}) async-start(), calls=%async_computation.13 | async-start | bytes 2654208 | tf_op jit(solution)/shard_map/all_gather | solution.py:49
  140.0 189.2 %all-gather.13.cloned.1.call-start = ((), (), s32[]{:S(2)}) async-start(), calls=%async_computation.12 | async-start | bytes 5242880 | tf_op jit(solution)/shard_map/all_gather | solution.py:84
  218.0 140.7 %all-gather.17.cloned.1.call-start = ((), (), s32[]{:S(2)}) async-start(), calls=%async_computation.14 | async-start | bytes 2654208 | tf_op jit(solution)/shard_map/all_gather | solution.py:50
  218.6 171.5 %all-gather.19.cloned.1.call-start = ((), (), s32[]{:S(2)}) async-start(), calls=%async_computation.15 | async-start | bytes 2654208 | tf_op jit(solution)/shard_map/all_gather | solution.py:51
  219.3 253.2 %all-gather.21.cloned.1.call-start = ((), (), s32[]{:S(2)}) async-start(), calls=%async_computation.17 | async-start | bytes 5242880 | tf_op jit(solution)/shard_map/all_gather | solution.py:98
  220.1 361.3 %reduce-scatter.12.cloned.1.call-start = ((), (), s32[]{:S(2)}) async-start(), calls=%async_computation.18 | async-start | bytes 5242880 | tf_op jit(solution)/shard_map/reduce_scatter | solution.py:112
  472.5 17.8 %copy-start.25 = (bf16[1024,1152]{1,0:T(8,128)(2,1)S(1)}, bf16[1024,1152]{1,0:T(8,128)(2,1)}, u32[]{:S(2)}) copy-start(bf16[1024,1152]{1,0:T(8,128)(2,1)} %all-gather.15.cloned.1.call-done) | copy-start | bytes 7077892
  505.9 77.7 %copy-start.10 = (bf16[512,1024]{1,0:T(8,128)(2,1)S(1)}, bf16[512,1024]{1,0:T(8,128)(2,1)}, u32[]{:S(2)}) copy-start(bf16[512,1024]{1,0:T(8,128)(2,1)} %param.19) | copy-start | bytes 3145732
  505.9 160.9 %all-gather.23.cloned.1.call-start = ((), (), s32[]{:S(2)}) async-start(), calls=%async_computation.19 | async-start | bytes 5242880 | tf_op jit(solution)/shard_map/all_gather | solution.py:117
  585.4 184.3 %reduce-scatter.14.cloned.1.call-start = ((), (), s32[]{:S(2)}) async-start(), calls=%async_computation.20 | async-start | bytes 5242880 | tf_op jit(solution)/shard_map/reduce_scatter | solution.py:139
  682.5 156.0 %reduce-scatter.10.cloned.1.call-start = ((), (), s32[]{:S(2)}) async-start(), calls=%async_computation.16 | async-start | bytes 5242880 | tf_op jit(solution)/shard_map/reduce_scatter | solution.py:91
  692.1 204.9 %reduce-scatter.16.cloned.1.call-start = ((), (), s32[]{:S(2)}) async-start(), calls=%async_computation.21 | async-start | bytes 5308416 | tf_op jit(solution)/shard_map/reduce_scatter | solution.py:106
  702.8 252.3 %reduce-scatter.18.cloned.1.call-start = ((), (), s32[]{:S(2)}) async-start(), calls=%async_computation.22 | async-start | bytes 5308416 | tf_op jit(solution)/shard_map/reduce_scatter | solution.py:107
  713.2 299.7 %reduce-scatter.20.cloned.1.call-start = ((), (), s32[]{:S(2)}) async-start(), calls=%async_computation.23 | async-start | bytes 5308416 | tf_op jit(solution)/shard_map/reduce_scatter | solution.py:108
  727.8 14.1 %all-to-all-start.1 = ((bf16[8,256,128]{2,1,0:T(8,128)(2,1)}), bf16[8,256,128]{2,1,0:T(8,128)(2,1)}, u32[]{:S(2)}, u32[]{:S(2)}) async-start(bf16[8,256,128]{2,1,0:T(8,128)(2,1)} %bitcast.76), calls=%async_computation.5 | async-start | bytes 1048576 | tf_op jit(solution)/shard_map/all_to_all | solution.py:19
  741.9 25.4 %all-to-all-start = ((bf16[8,128,3,256]{3,1,2,0:T(8,128)(2,1)}), bf16[8,128,3,256]{3,1,2,0:T(8,128)(2,1)}, u32[]{:S(2)}, u32[]{:S(2)}) async-start(bf16[8,128,3,256]{3,1,2,0:T(8,128)(2,1)} %copy.22), calls=%async_computation.4 | async-start | bytes 3145728 | tf_op jit(solution)/shard_map/all_to_all | solution.py:19
  746.2 23.5 %copy-start.20 = (f32[1024]{0:T(1024)S(1)}, f32[1024]{0:T(1024)}, u32[]{:S(2)}) copy-start(f32[1024]{0:T(1024)} %copy-done.19) | copy-start | bytes 12292
  746.2 23.5 %copy-start.23 = (f32[512]{0:T(512)S(1)}, f32[512]{0:T(512)}, u32[]{:S(2)}) copy-start(f32[512]{0:T(512)} %copy-done.22) | copy-start | bytes 6148
  (22 other events, 69.4 us)
Sparse Core Ops, SparseCore 0:
  9.9 29.0 all-gather.10
  41.2 80.7 all-gather.8
  139.5 75.2 reduce-scatter.7
  216.7 29.5 all-gather.14
  248.4 80.7 all-gather.12
  331.1 27.5 all-gather.16
  360.7 29.3 all-gather.18
  391.7 80.7 all-gather.20
  506.0 75.2 reduce-scatter.11
  585.5 81.2 all-gather.22
  682.6 75.2 reduce-scatter.13
  760.2 78.3 reduce-scatter.9
  842.6 54.3 reduce-scatter.15
  901.2 53.8 reduce-scatter.17
  959.0 53.8 reduce-scatter.19
where the time goes:
time: 1030 us; the launch traced here: 1020 us
  waiting for transfers between devices  778 us (76%)
  matrix products  124 us (12%)
  blocking collectives  55.3 us (5%)
  other arithmetic  27.3 us (3%)
  between operations  14.4 us (1%)
  local copies, waits for them, and re-layouts  11.2 us (1%)
    all_gather x1, waiting for transfers between devices, body(): first_all = lax.all_gather(first, 'tensor', axis=0, tiled=True)  82.9 us
    all_gather x1, waiting for transfers between devices, body(): second_all = lax.all_gather(second, 'tensor', axis=0, tiled=True)  82.9 us
    all_gather x1, waiting for transfers between devices, body(): cot_all = lax.all_gather(d_out, 'tensor', axis=0, tiled=True)  82.4 us
    all_gather x1, waiting for transfers between devices, body(): lax.all_gather(d_resid.astype(jnp.bfloat16), 'tensor', axis=0, tiled=True)  81.4 us
    reduce_scatter x1, waiting for transfers between devices, body(): lax.psum_scatter((part_gate + part_up).astype(jnp.bfloat16), 'tensor', sc...  75.4 us
    reduce_scatter x1, waiting for transfers between devices, body(): lax.psum_scatter(jnp.dot(rows_now, out_full, preferred_element_type=jnp.f...  74.8 us
    reduce_scatter x1, waiting for transfers between devices, body(): lax.psum_scatter(grad_up, 'dp', scatter_dimension=0, tiled=True)  58.2 us
    reduce_scatter x1, waiting for transfers between devices, body(): lax.psum_scatter(grad_down, 'dp', scatter_dimension=1, tiled=True)  57.8 us
  transfers between devices with their start and end apart: 17, of which 16 were waited for; matrix products, arithmetic and copies ran while one was open for 9% of the time, Pallas kernels for 0%

commit v1 on v0

v1 whole, which is shorter than its diff:
```python
import jax
import jax.numpy as jnp
import numpy as np
from jax import lax
from jax.sharding import PartitionSpec as P

LEN = 1024
epsilon = 1e-05
AXES = ("dp", "tensor")
bf16 = jnp.bfloat16
f32 = jnp.float32


class Links:
    def __init__(self, dp, tensor):
        self.dp, self.tensor = dp, tensor
        self.bits = (dp // 2).bit_length() - 1
        assert dp == 2 << self.bits
        self.devices = [(d, t) for d in range(dp) for t in range(tensor)]

    def at(self, d, t):
        return d * self.tensor + t

    def pairs(self, target):
        return [(self.at(d, t), self.at(*target(d, t))) for d, t in self.devices]

    def shift(self, k):
        return self.pairs(lambda d, t: (d, (t - k) % self.tensor))

    def flip(self, core, step):
        return 2 << (step if core == 0 else self.bits - 1 - step)

    def step(self, j):
        return self.pairs(lambda d, t: (d ^ self.flip(d % 2, j), t))

    def cores(self):
        return self.pairs(lambda d, t: (d ^ 1, t))

    def order(self):
        table = np.zeros((self.dp, self.dp), np.int32)
        half = self.dp // 2
        for d in range(self.dp):
            for p in range(self.dp):
                source = d ^ 1 if p >= half else d
                for j in range(self.bits):
                    if (p >> j) & 1:
                        source ^= self.flip(source % 2, j)
                table[d, p] = source
        return table


def send(x, pairs):
    return lax.ppermute(x, AXES, pairs)


def gather(links, x, order):
    step = 0
    for name in order:
        if name == "z":
            x = jnp.concatenate([x] + [send(x, links.shift(k)) for k in range(1, links.tensor)], axis=1)
        else:
            x = jnp.concatenate([x, send(x, links.step(step))], axis=0)
            step += 1
    return x, send(x, links.cores())


def scatter_sum(links, own, other):
    x = own.astype(f32) + send(other, links.cores()).astype(f32)
    for j in reversed(range(links.bits)):
        half = x.shape[0] // 2
        away = x[half:].astype(bf16)
        x = x[:half] + send(away, links.step(j)).astype(f32)
    n = x.shape[1] // links.tensor
    total = x[:, :n]
    for k in range(1, links.tensor):
        back = [(b, a) for a, b in links.shift(k)]
        total = total + send(x[:, k * n : (k + 1) * n].astype(bf16), back).astype(f32)
    return total


def sum_all(links, x):
    x = x + send(x, links.cores())
    for j in range(links.bits):
        x = x + send(x, links.step(j))
    k = 1
    while k < links.tensor:
        x = x + send(x, links.pairs(lambda d, t: (d, t ^ k)))
        k *= 2
    return x


def dot(a, b, ca, cb):
    return lax.dot_general(a, b, (((ca,), (cb,)), ((), ())), preferred_element_type=f32)


def norm_rows(values):
    scale = lax.rsqrt(jnp.mean(values * values, axis=-1, keepdims=True) + epsilon)
    return (values * scale, scale)


def norm_back(grad_h, normed, scale, gain):
    grad_n = grad_h * gain
    inner = jnp.mean(grad_n * normed, axis=-1, keepdims=True)
    return scale * (grad_n - normed * inner)


def make_body(links):
    dp, T = links.dp, links.tensor
    table = links.order()

    def body(x_in, in_w, out_w, gate_w, up_w, down_w, conv_w, gain1, gain2, d_out):
        rows, D = x_in.shape
        block = D // dp
        half = D // 2
        chan = in_w.shape[2]
        C = chan * T
        FF = gate_w.shape[1] * T
        per_seq = LEN // rows
        me_dp = lax.axis_index("dp")
        me_t = lax.axis_index("tensor")

        conv_blocks = jnp.concatenate([in_w.reshape(block, 3 * chan), out_w.T], axis=1)
        stages = ["x"] * links.bits
        conv0, conv1 = gather(links, conv_blocks, ["z"] + stages)
        gate0, gate1 = gather(links, gate_w, ["z"] + stages)
        up0, up1 = gather(links, up_w, ["z"] + stages)
        down0, down1 = gather(links, down_w.T, ["z"] + stages)

        def split_conv(w):
            w = w.reshape(half, T, 4, chan)
            return [w[:, :, k].reshape(half, C) for k in range(4)]

        b0, c0, x0, out0 = split_conv(conv0)
        b1, c1, x1, out1 = split_conv(conv1)

        mine = jnp.take(jnp.asarray(table), me_dp, axis=0)
        source = (mine[:, None] * block + jnp.arange(block)[None, :]).reshape(D)
        place = (jnp.arange(D)[:, None] == source[None, :]).astype(bf16)

        def arrange(v):
            return dot(v, place, 1, 0).astype(bf16)

        def restore(v):
            return dot(v, place, 1, 1).astype(bf16)

        def restore_rows(v):
            return jnp.sum(
                jnp.where((mine[None, :] == jnp.arange(dp)[:, None])[:, :, None], v.reshape(1, dp, block), 0.0), axis=1
            ).reshape(D)

        tokens = arrange(x_in).astype(f32)
        cot16 = arrange(d_out)
        gains = arrange(jnp.stack([gain1, gain2])).astype(f32)
        gain_one, gain_two = gains[0], gains[1]
        turned = jnp.concatenate([conv_w, conv_w], axis=1)
        kernel = lax.dynamic_slice_in_dim(turned, me_t * chan, C, 1).astype(f32)

        normed_one, scale_one = norm_rows(tokens)
        first = (normed_one * gain_one).astype(bf16)

        def proj(a, w0, w1):
            return dot(a[:, :half], w0, 1, 0) + dot(a[:, half:], w1, 1, 0)

        def proj_t(a, w0, w1):
            return jnp.concatenate([dot(a, w0, 1, 1), dot(a, w1, 1, 1)], axis=1)

        b_part = proj(first, b0, b1)
        c_part = proj(first, c0, c1)
        x_part = proj(first, x0, x1)
        mixed_in = b_part * x_part
        follows = [(links.at(d, t), links.at(d, t + 1)) for d, t in links.devices if (t + 1) % per_seq]
        before = send(jnp.roll(mixed_in[rows - 2 :], -chan, axis=1), follows) if follows else jnp.zeros((2, C), f32)
        lead = jnp.concatenate([before, mixed_in[: rows - 1]], axis=0)
        back_one = lead[1:]
        back_two = lead[:rows]
        conv_out = kernel[2] * mixed_in + kernel[1] * back_one + kernel[0] * back_two
        branch = (c_part * conv_out).astype(bf16)
        resid = tokens + proj_t(branch, out0, out1)
        normed_two, scale_two = norm_rows(resid)
        second = (normed_two * gain_two).astype(bf16)
        gate = proj(second, gate0, gate1)
        up_val = proj(second, up0, up1)
        sigma = jax.nn.sigmoid(gate)
        silu_gate = gate * sigma
        hidden = (silu_gate * up_val).astype(bf16)

        def weight_grad(a, b):
            return dot(a[:, :half], b, 0, 0).astype(bf16), dot(a[:, half:], b, 0, 0).astype(bf16)

        grad_down = scatter_sum(links, *weight_grad(cot16, hidden)).T
        d_hidden = proj(cot16, down0, down1)
        d_gate = (d_hidden * up_val * sigma * (1.0 + gate * (1.0 - sigma))).astype(bf16)
        d_up = (d_hidden * silu_gate).astype(bf16)
        grad_gate = scatter_sum(links, *weight_grad(second, d_gate))
        grad_up = scatter_sum(links, *weight_grad(second, d_up))
        d_second = proj_t(d_gate, gate0, gate1) + proj_t(d_up, up0, up1)
        gain_two_part = jnp.sum(d_second * normed_two, axis=0)
        d_resid = cot16.astype(f32) + norm_back(d_second, normed_two, scale_two, gain_two)
        d_mixed = d_resid.astype(bf16)
        d_branch = proj(d_mixed, out0, out1)
        grad_out = scatter_sum(links, *weight_grad(d_mixed, branch)).T
        d_conv = d_branch * c_part
        d_c = d_branch * conv_out
        leads = [(b, a) for a, b in follows]
        after = send(jnp.roll(d_conv[:2], chan, axis=1), leads) if leads else jnp.zeros((2, C), f32)
        trail = jnp.concatenate([d_conv[1:], after], axis=0)
        d_mixin = kernel[2] * d_conv + kernel[1] * trail[:rows] + kernel[0] * trail[1:]
        taps = [jnp.sum(d_conv * v, axis=0) for v in (back_two, back_one, mixed_in)]
        d_b = (d_mixin * x_part).astype(bf16)
        d_c = d_c.astype(bf16)
        d_xpart = (d_mixin * b_part).astype(bf16)
        grads_in = [scatter_sum(links, *weight_grad(first, v)) for v in (d_b, d_c, d_xpart)]
        grad_in = jnp.stack(grads_in, axis=1)
        d_first = proj_t(d_b, b0, b1) + proj_t(d_c, c0, c1) + proj_t(d_xpart, x0, x1)
        gain_one_part = jnp.sum(d_first * normed_one, axis=0)
        d_x = restore((d_resid + norm_back(d_first, normed_one, scale_one, gain_one)).astype(bf16))
        block_out = restore((resid + proj_t(hidden, down0, down1)).astype(bf16))

        taps = jnp.stack(taps)
        taps = lax.dynamic_slice_in_dim(jnp.concatenate([taps, taps], axis=1), C - me_t * chan, C, 1)
        small = jnp.concatenate([taps, restore_rows(gain_one_part)[None], restore_rows(gain_two_part)[None]], axis=0)
        small = sum_all(links, small)
        return (
            block_out,
            d_x,
            grad_in,
            grad_out,
            grad_gate,
            grad_up,
            grad_down,
            small[:3],
            small[3],
            small[4],
        )

    return body


def solution(mesh):
    links = Links(mesh.shape["dp"], mesh.shape["tensor"])
    in_specs = (
        P(("dp", "tensor"), None),
        P("dp", None, "tensor"),
        P("tensor", "dp"),
        P("dp", "tensor"),
        P("dp", "tensor"),
        P("tensor", "dp"),
        P(),
        P(),
        P(),
        P(("dp", "tensor"), None),
    )
    out_specs = (
        P(("dp", "tensor"), None),
        P(("dp", "tensor"), None),
        P("dp", None, "tensor"),
        P("tensor", "dp"),
        P("dp", "tensor"),
        P("dp", "tensor"),
        P("tensor", "dp"),
        P(),
        P(),
        P(),
    )
    return jax.shard_map(
        make_body(links), mesh=mesh, in_specs=in_specs, out_specs=out_specs, check_vma=False
    )
```

time: 1030 us -> 640 us (0.62)
  waiting for transfers between devices: 778 us -> 250 us
  starting transfers between devices: 9.41 us -> 132 us
  blocking collectives: 55.3 us -> 0 us
  other arithmetic: 27.3 us -> 65.2 us
  local copies, waits for them, and re-layouts: 11.2 us -> 47.9 us
  matrix products: 124 us -> 137 us
  between operations: 14.4 us -> 2.45 us
    all_gather x8 -> x0, waiting for transfers between devices: 409 us -> none  [the longest x1 82.9 us: body(): first_all = lax.all_gather(first, 'tensor', axis=0, tiled=True)]
    reduce_scatter x7 -> x0, waiting for transfers between devices: 345 us -> none  [the longest x1 75.4 us: body(): lax.psum_scatter((part_gate + part_up).astype(jnp.bfloat16), 'tensor', sc...]
    ppermute x0 -> x73, waiting for transfers between devices: none -> 250 us  [send(): return lax.ppermute(x, AXES, pairs)]
    ppermute x0 -> x73, starting transfers between devices: none -> 132 us  [send(): return lax.ppermute(x, AXES, pairs)]
    psum x1 -> x0, blocking collectives: 42.6 us -> none  [body(): lax.psum((gain_one_part, gain_two_part, taps_whole), ('dp', 'tensor'))]
    concatenate x0 -> x14, other arithmetic: none -> 36.6 us  [the longest x8 34.8 us: gather(): x = jnp.concatenate([x, send(x, links.step(step))], axis=0)]
    all_to_all x2 -> x0, waiting for transfers between devices: 20.9 us -> none  [sum_at_owner(): lax.all_to_all(tiles, axis, split_axis=0, concat_axis=0, tiled=True)]
    unnamed x58 -> x195, local copies, waits for them, and re-layouts: 8.58 us -> 29.1 us
  transfers between devices with their start and end apart: 17 -> 73, of which waited for: 16 -> 35; matrix products, arithmetic and copies ran while one was open for 9% -> 24% of each run, Pallas kernels for 0% -> 0%
where the time goes in v1:
time: 640 us; the launch traced here: 634 us
  waiting for transfers between devices  250 us (39%)
  matrix products  137 us (21%)
  starting transfers between devices  132 us (21%)
  other arithmetic  65.2 us (10%)
  local copies, waits for them, and re-layouts  47.9 us (7%)
    ppermute x73, waiting for transfers between devices, send(): return lax.ppermute(x, AXES, pairs)  250 us
    dot_general x47, matrix products, dot(): lax.dot_general(a, b, (((ca,), (cb,)), ((), ())), preferred_element_type=...  137 us
    ppermute x73, starting transfers between devices, send(): return lax.ppermute(x, AXES, pairs)  132 us
    concatenate x8, other arithmetic, gather(): x = jnp.concatenate([x, send(x, links.step(step))], axis=0)  34.8 us
    unnamed x195, local copies, waits for them, and re-layouts  29.1 us
  transfers between devices with their start and end apart: 73, of which 35 were waited for; matrix products, arithmetic and copies ran while one was open for 24% of the time, Pallas kernels for 0%

profile of v1, /device:TPU:0, one launch (start us, length us, event | category | flops | bytes accessed | tf_op | source)
XLA Modules:
  0.0 634.1 jit_solution(5993388641577005936)
XLA Ops:
  32.8 9.0 %collective-permute-start.13 = (bf16[128,1152]{1,0:T(8,128)(2,1)}, bf16[128,1152]{1,0:T(8,128)(2,1)S(1)}, u32[]{:S(2)}, u32[]{:S(2)}) collective-permute-start(bf16[128,1152]{1,0:T(8,128)(2,1)} %param.15), channel_id=1, source_target_pairs={{0,3},{1,0},{2,1},{3,2},{4,7},{5,4},{6,5},{7,6},{8,11},{9,8},{10,9... | collective-permute-start | bytes 884744 | tf_op jit(solution)/shard_map/ppermute | solution.py:53
  53.0 10.8 %collective-permute-done.8 = bf16[128,1152]{1,0:T(8,128)(2,1)} collective-permute-done((bf16[128,1152]{1,0:T(8,128)(2,1)}, bf16[128,1152]{1,0:T(8,128)(2,1)}, u32[]{:S(2)}, u32[]{:S(2)}) %collective-permute-start.8) | collective-permute-done | bytes 294944 | tf_op jit(solution)/shard_map/ppermute | solution.py:53
  72.2 10.5 %collective-permute-done.14 = bf16[128,1152]{1,0:T(8,128)(2,1)S(1)} collective-permute-done((bf16[128,1152]{1,0:T(8,128)(2,1)S(1)}, bf16[128,1152]{1,0:T(8,128)(2,1)S(1)}, u32[]{:S(2)}, u32[]{:S(2)}) %collective-permute-start.14) | collective-permute-done | bytes 294944 | tf_op jit(solution)/shard_map/ppermute | solution.py:53
  82.7 13.3 %collective-permute-start.21 = (bf16[128,1152]{0,1:T(8,128)(2,1)S(1)}, bf16[128,1152]{0,1:T(8,128)(2,1)S(1)}, u32[]{:S(2)}, u32[]{:S(2)}) collective-permute-start(bf16[128,1152]{0,1:T(8,128)(2,1)S(1)} %bitcast.178), channel_id=1, source_target_pairs={{0,1},{1,2},{2,3},{3,0},{4,5},{5,6},{6,7},{7,4},{8,9},{9,10},{10,1... | collective-permute-start | bytes 884744 | tf_op jit(solution)/shard_map/ppermute | solution.py:53
  97.6 9.2 %collective-permute-done.20 = bf16[128,1152]{0,1:T(8,128)(2,1)S(1)} collective-permute-done((bf16[128,1152]{0,1:T(8,128)(2,1)S(1)}, bf16[128,1152]{0,1:T(8,128)(2,1)S(1)}, u32[]{:S(2)}, u32[]{:S(2)}) %collective-permute-start.20) | collective-permute-done | bytes 294944 | tf_op jit(solution)/shard_map/ppermute | solution.py:53
  126.8 21.0 %collective-permute-done.22 = bf16[128,4608]{0,1:T(8,128)(2,1)S(1)} collective-permute-done((bf16[128,4608]{0,1:T(8,128)(2,1)S(1)}, bf16[128,4608]{0,1:T(8,128)(2,1)S(1)}, u32[]{:S(2)}, u32[]{:S(2)}) %collective-permute-start.22) | collective-permute-done | bytes 1179680 | tf_op jit(solution)/shard_map/ppermute | solution.py:53
  147.8 9.7 %pad_maximum_fusion.6 = bf16[256,4608]{0,1:T(8,128)(2,1)} fusion(bf16[128,4608]{0,1:T(8,128)(2,1)S(1)} %collective-permute-done.22, bf16[128,1152]{0,1:T(8,128)(2,1)S(1)} %collective-permute-done.21, bf16[128,1152]{0,1:T(8,128)(2,1)S(1)} %collective-permute-done.20, bf16[128,1152]{0,1:T(8,128)(2,1)S(1)} %collective-permute-done.19, ...), kind=kLoop, calls=%fused_computation.42 | loop fusion | flops 11796480 | bytes 4718592 | tf_op jit(solution)/shard_map/concatenate | solution.py:62
  169.1 12.7 %collective-permute-done.17 = bf16[256,4608]{1,0:T(8,128)(2,1)} collective-permute-done((bf16[256,4608]{1,0:T(8,128)(2,1)}, bf16[256,4608]{1,0:T(8,128)(2,1)}, u32[]{:S(2)}, u32[]{:S(2)}) %collective-permute-start.17) | collective-permute-done | bytes 2359328 | tf_op jit(solution)/shard_map/ppermute | solution.py:53
  185.4 21.6 %collective-permute-done.23 = bf16[256,4608]{0,1:T(8,128)(2,1)} collective-permute-done((bf16[256,4608]{0,1:T(8,128)(2,1)}, bf16[256,4608]{0,1:T(8,128)(2,1)}, u32[]{:S(2)}, u32[]{:S(2)}) %collective-permute-start.23) | collective-permute-done | bytes 2359328 | tf_op jit(solution)/shard_map/ppermute | solution.py:53
  207.0 12.1 %pad_maximum_fusion.2 = bf16[512,4608]{0,1:T(8,128)(2,1)S(1)} fusion(bf16[256,4608]{0,1:T(8,128)(2,1)} %collective-permute-done.23, bf16[128,4608]{0,1:T(8,128)(2,1)S(1)} %copy-done.32, bf16[128,1152]{0,1:T(8,128)(2,1)S(1)} %copy-done.62, bf16[128,1152]{0,1:T(8,128)(2,1)S(1)} %copy-done.60, bf16[128,1152]{0,1:T(8,128)(2,1)S(1)} %copy-done.58, ...), kind=kLoop, calls=%fused_computation.25 | loop fusion | flops 28311552 | bytes 9437184 | tf_op jit(solution)/shard_map/concatenate | solution.py:62
  227.9 7.0 %collective-permute-start.6 = (f32[2,1024]{1,0:T(2,128)S(1)}, f32[2,1024]{1,0:T(2,128)S(1)}, u32[]{:S(2)}, u32[]{:S(2)}) collective-permute-start(f32[2,1024]{1,0:T(2,128)S(1)} %pad_maximum_fusion.14), channel_id=1, source_target_pairs={{0,1},{2,3},{4,5},{6,7},{8,9},{10,11},{12,13},{14,15},{16,17},{18,... | collective-permute-start | bytes 24584 | tf_op jit(solution)/shard_map/ppermute | solution.py:53
  263.7 8.2 %convolution_add_fusion.1 = f32[512,4608]{1,0:T(8,128)} fusion(f32[512,4608]{1,0:T(8,128)S(1)} %fusion.72, bf16[512,1024]{0,1:T(8,128)(2,1)S(1)} %multiply_convert_fusion.6, bf16[256,4608]{1,0:T(8,128)(2,1)} %collective-permute-done.17, bf16[128,4608]{1,0:T(8,128)(2,1)S(1)} %copy-done.14, bf16[128,4608]{1,0:T(8,128)(2,1)S(1)} %copy-done.11), kind=kOutput, calls=%fused_computation.9 | convolution fusion | flops 2432434176 | bytes 24117248 | tf_op jit(solution)/shard_map/dot_general | solution.py:93
  271.9 17.8 %multiply_convert_fusion.1 = (bf16[512,4608]{1,0:T(8,128)(2,1)}, bf16[512,4608]{1,0:T(8,128)(2,1)}, bf16[512,4608]{1,0:T(8,128)(2,1)}) fusion(f32[512,4608]{1,0:T(8,128)} %convolution_add_fusion, f32[512,4608]{1,0:T(8,128)} %convolution_add_fusion.1, f32[512,4608]{1,0:T(8,128)} %fusion.74, bf16[256,4608]{1,0:T(8,128)(2,1)} %collective-permute-done.11, ...), kind=kOutput, calls=%fused_computation.4 | convolution fusion | flops 2467823616 | bytes 47710208 | tf_op jit(solution)/shard_map/dot_general | solution.py:93
  289.7 6.5 %fusion.135 = f32[512,512]{0,1:T(8,128)S(1)} fusion(bf16[512,4608]{1,0:T(8,128)(2,1)} %get-tuple-element.94, bf16[256,4608]{1,0:T(8,128)(2,1)} %collective-permute-done.11, bf16[128,4608]{1,0:T(8,128)(2,1)} %copy-done.29, bf16[128,4608]{1,0:T(8,128)(2,1)} %copy-done.24), kind=kOutput, calls=%fused_computation.255 | convolution fusion | flops 2430074880 | bytes 10485760 | tf_op jit(solution)/shard_map/dot_general | solution.py:93
  386.2 6.1 collective-permute-done.45
  405.3 6.7 %collective-permute-done.39 = bf16[256,1024]{1,0:T(8,128)(2,1)S(1)} collective-permute-done((bf16[256,1024]{1,0:T(8,128)(2,1)S(1)}, bf16[256,1024]{1,0:T(8,128)(2,1)S(1)}, u32[]{:S(2)}, u32[]{:S(2)}) %collective-permute-start.39) | collective-permute-done | bytes 524320 | tf_op jit(solution)/shard_map/ppermute | solution.py:53
  464.5 5.9 convert_add_fusion.1
  474.2 6.4 %convert_add_fusion.2 = f32[512,4608]{1,0:T(8,128)S(1)} fusion(bf16[512,4608]{1,0:T(8,128)(2,1)} %collective-permute-done.50, bf16[512,4608]{1,0:T(8,128)(2,1)} %get-tuple-element.94, bf16[512,1024]{0,1:T(8,128)(2,1)S(1)} %copy-done.9), kind=kOutput, calls=%fused_computation.2 | convolution fusion | flops 2425356288 | bytes 19398656 | tf_op jit(solution)/shard_map/dot_general | solution.py:93
  489.8 38.8 %collective-permute-done.57 = bf16[256,4608]{1,0:T(8,128)(2,1)} collective-permute-done((bf16[256,4608]{1,0:T(8,128)(2,1)}, bf16[256,4608]{1,0:T(8,128)(2,1)}, u32[]{:S(2)}, u32[]{:S(2)}) %collective-permute-start.57) | collective-permute-done | bytes 2359328 | tf_op jit(solution)/shard_map/ppermute | solution.py:53
  532.6 38.6 %collective-permute-done.51 = bf16[256,4608]{1,0:T(8,128)(2,1)} collective-permute-done((bf16[256,4608]{1,0:T(8,128)(2,1)}, bf16[256,4608]{1,0:T(8,128)(2,1)}, u32[]{:S(2)}, u32[]{:S(2)}) %collective-permute-start.51) | collective-permute-done | bytes 2359328 | tf_op jit(solution)/shard_map/ppermute | solution.py:53
  582.6 7.3 %collective-permute-done.52 = bf16[128,4608]{1,0:T(8,128)(2,1)S(1)} collective-permute-done((bf16[128,4608]{1,0:T(8,128)(2,1)S(1)}, bf16[128,4608]{1,0:T(8,128)(2,1)S(1)}, u32[]{:S(2)}, u32[]{:S(2)}) %collective-permute-start.52) | collective-permute-done | bytes 1179680 | tf_op jit(solution)/shard_map/ppermute | solution.py:53
  592.8 7.8 %collective-permute-done.66 = bf16[128,1152]{1,0:T(8,128)(2,1)S(1)} collective-permute-done((bf16[128,1152]{1,0:T(8,128)(2,1)S(1)}, bf16[128,1152]{1,0:T(8,128)(2,1)S(1)}, u32[]{:S(2)}, u32[]{:S(2)}) %collective-permute-start.66) | collective-permute-done | bytes 294944 | tf_op jit(solution)/shard_map/ppermute | solution.py:53
  600.6 10.9 %collective-permute-start.53 = (bf16[128,1152]{1,0:T(8,128)(2,1)}, bf16[128,1152]{1,0:T(8,128)(2,1)}, u32[]{:S(2)}, u32[]{:S(2)}) collective-permute-start(bf16[128,1152]{1,0:T(8,128)(2,1)} %get-tuple-element.112), channel_id=1, source_target_pairs={{3,0},{0,1},{1,2},{2,3},{7,4},{4,5},{5,6},{6,7},{11,8},{8,9},{9,10... | collective-permute-start | bytes 884744 | tf_op jit(solution)/shard_map/ppermute | solution.py:53
  619.2 6.2 collective-permute-done.60
  (467 shorter events, 327.6 us)
Async XLA Ops:
  9.5 37.9 %collective-permute-start.7 = (bf16[128,1152]{1,0:T(8,128)(2,1)}, bf16[128,1152]{1,0:T(8,128)(2,1)}, u32[]{:S(2)}, u32[]{:S(2)}) collective-permute-start(bf16[128,1152]{1,0:T(8,128)(2,1)} %param.14), channel_id=1, source_target_pairs={{0,3},{1,0},{2,1},{3,2},{4,7},{5,4},{6,5},{7,6},{8,11},{9,8},{10,9... | collective-permute-start | bytes 884744 | tf_op jit(solution)/shard_map/ppermute | solution.py:53
  12.3 51.5 %collective-permute-start.8 = (bf16[128,1152]{1,0:T(8,128)(2,1)}, bf16[128,1152]{1,0:T(8,128)(2,1)}, u32[]{:S(2)}, u32[]{:S(2)}) collective-permute-start(bf16[128,1152]{1,0:T(8,128)(2,1)} %param.14), channel_id=1, source_target_pairs={{0,2},{1,3},{2,0},{3,1},{4,6},{5,7},{6,4},{7,5},{8,10},{9,11},{10,... | collective-permute-start | bytes 884744 | tf_op jit(solution)/shard_map/ppermute | solution.py:53
  20.8 48.1 %collective-permute-start.9 = (bf16[128,1152]{1,0:T(8,128)(2,1)}, bf16[128,1152]{1,0:T(8,128)(2,1)S(1)}, u32[]{:S(2)}, u32[]{:S(2)}) collective-permute-start(bf16[128,1152]{1,0:T(8,128)(2,1)} %param.14), channel_id=1, source_target_pairs={{0,1},{1,2},{2,3},{3,0},{4,5},{5,6},{6,7},{7,4},{8,9},{9,10},{10,1... | collective-permute-start | bytes 884744 | tf_op jit(solution)/shard_map/ppermute | solution.py:53
  32.8 37.8 %collective-permute-start.13 = (bf16[128,1152]{1,0:T(8,128)(2,1)}, bf16[128,1152]{1,0:T(8,128)(2,1)S(1)}, u32[]{:S(2)}, u32[]{:S(2)}) collective-permute-start(bf16[128,1152]{1,0:T(8,128)(2,1)} %param.15), channel_id=1, source_target_pairs={{0,3},{1,0},{2,1},{3,2},{4,7},{5,4},{6,5},{7,6},{8,11},{9,8},{10,9... | collective-permute-start | bytes 884744 | tf_op jit(solution)/shard_map/ppermute | solution.py:53
  69.0 45.7 %collective-permute-start.4 = (bf16[256,4096]{0,1:T(8,128)(2,1)S(1)}, bf16[256,4096]{0,1:T(8,128)(2,1)S(1)}, u32[]{:S(2)}, u32[]{:S(2)}) collective-permute-start(bf16[256,4096]{0,1:T(8,128)(2,1)S(1)} %pad_maximum_fusion.9), channel_id=1, source_target_pairs={{0,16},{1,17},{2,18},{3,19},{4,12},{5,13},{6,14},{7,15},{8,24},{9,... | collective-permute-start | bytes 6291464 | tf_op jit(solution)/shard_map/ppermute | solution.py:53
  70.6 37.9 %collective-permute-start.10 = (bf16[128,4608]{1,0:T(8,128)(2,1)S(1)}, bf16[128,4608]{1,0:T(8,128)(2,1)S(1)}, u32[]{:S(2)}, u32[]{:S(2)}) collective-permute-start(bf16[128,4608]{1,0:T(8,128)(2,1)S(1)} %constant_dynamic-update-slice_fusion.5), channel_id=1, source_target_pairs={{0,8},{1,9},{2,10},{3,11},{4,20},{5,21},{6,22},{7,23},{8,0},{9,1},... | collective-permute-start | bytes 3538952 | tf_op jit(solution)/shard_map/ppermute | solution.py:53
  106.9 40.9 %collective-permute-start.22 = (bf16[128,4608]{0,1:T(8,128)(2,1)S(1)}, bf16[128,4608]{0,1:T(8,128)(2,1)S(1)}, u32[]{:S(2)}, u32[]{:S(2)}) collective-permute-start(bf16[128,4608]{0,1:T(8,128)(2,1)S(1)} %pad_maximum_fusion.10), channel_id=1, source_target_pairs={{0,8},{1,9},{2,10},{3,11},{4,20},{5,21},{6,22},{7,23},{8,0},{9,1},... | collective-permute-start | bytes 3538952 | tf_op jit(solution)/shard_map/ppermute | solution.py:53
  110.1 55.0 %collective-permute-start.11 = (bf16[256,4608]{1,0:T(8,128)(2,1)}, bf16[256,4608]{1,0:T(8,128)(2,1)}, u32[]{:S(2)}, u32[]{:S(2)}) collective-permute-start(bf16[256,4608]{1,0:T(8,128)(2,1)} %pad_maximum_fusion.4), channel_id=1, source_target_pairs={{0,16},{1,17},{2,18},{3,19},{4,12},{5,13},{6,14},{7,15},{8,24},{9,... | collective-permute-start | bytes 7077896 | tf_op jit(solution)/shard_map/ppermute | solution.py:53
  117.1 102.1 %collective-permute-start.5 = (bf16[512,4096]{0,1:T(8,128)(2,1)}, bf16[512,4096]{0,1:T(8,128)(2,1)}, u32[]{:S(2)}, u32[]{:S(2)}) collective-permute-start(bf16[512,4096]{0,1:T(8,128)(2,1)} %pad_maximum_fusion.3), channel_id=1, source_target_pairs={{0,4},{1,5},{2,6},{3,7},{4,0},{5,1},{6,2},{7,3},{8,12},{9,13},{10,... | collective-permute-start | bytes 12582920 | tf_op jit(solution)/shard_map/ppermute | solution.py:53
  124.3 57.4 %collective-permute-start.17 = (bf16[256,4608]{1,0:T(8,128)(2,1)}, bf16[256,4608]{1,0:T(8,128)(2,1)}, u32[]{:S(2)}, u32[]{:S(2)}) collective-permute-start(bf16[256,4608]{1,0:T(8,128)(2,1)} %pad_maximum_fusion.5), channel_id=1, source_target_pairs={{0,16},{1,17},{2,18},{3,19},{4,12},{5,13},{6,14},{7,15},{8,24},{9,... | collective-permute-start | bytes 7077896 | tf_op jit(solution)/shard_map/ppermute | solution.py:53
  157.5 49.5 %collective-permute-start.23 = (bf16[256,4608]{0,1:T(8,128)(2,1)}, bf16[256,4608]{0,1:T(8,128)(2,1)}, u32[]{:S(2)}, u32[]{:S(2)}) collective-permute-start(bf16[256,4608]{0,1:T(8,128)(2,1)} %pad_maximum_fusion.6), channel_id=1, source_target_pairs={{0,16},{1,17},{2,18},{3,19},{4,12},{5,13},{6,14},{7,15},{8,24},{9,... | collective-permute-start | bytes 7077896 | tf_op jit(solution)/shard_map/ppermute | solution.py:53
  169.0 74.5 %collective-permute-start.12 = (bf16[512,4608]{1,0:T(8,128)(2,1)S(1)}, bf16[512,4608]{1,0:T(8,128)(2,1)S(1)}, u32[]{:S(2)}, u32[]{:S(2)}) collective-permute-start(bf16[512,4608]{1,0:T(8,128)(2,1)S(1)} %pad_maximum_fusion), channel_id=1, source_target_pairs={{0,4},{1,5},{2,6},{3,7},{4,0},{5,1},{6,2},{7,3},{8,12},{9,13},{10,... | collective-permute-start | bytes 14155784 | tf_op jit(solution)/shard_map/ppermute | solution.py:53
  185.4 73.7 %collective-permute-start.18 = (bf16[512,4608]{1,0:T(8,128)(2,1)}, bf16[512,4608]{1,0:T(8,128)(2,1)}, u32[]{:S(2)}, u32[]{:S(2)}) collective-permute-start(bf16[512,4608]{1,0:T(8,128)(2,1)} %pad_maximum_fusion.1), channel_id=1, source_target_pairs={{0,4},{1,5},{2,6},{3,7},{4,0},{5,1},{6,2},{7,3},{8,12},{9,13},{10,... | collective-permute-start | bytes 14155784 | tf_op jit(solution)/shard_map/ppermute | solution.py:53
  339.3 101.4 %collective-permute-start.62 = (bf16[512,4608]{1,0:T(8,128)(2,1)}, bf16[512,4608]{1,0:T(8,128)(2,1)}, u32[]{:S(2)}, u32[]{:S(2)}) collective-permute-start(bf16[512,4608]{1,0:T(8,128)(2,1)} %convolution_convert_fusion), channel_id=1, source_target_pairs={{0,4},{1,5},{2,6},{3,7},{4,0},{5,1},{6,2},{7,3},{8,12},{9,13},{10,... | collective-permute-start | bytes 14155784 | tf_op jit(solution)/shard_map/ppermute | solution.py:53
  339.3 39.0 %collective-permute-start.44 = (bf16[512,1024]{1,0:T(8,128)(2,1)}, bf16[512,1024]{1,0:T(8,128)(2,1)}, u32[]{:S(2)}, u32[]{:S(2)}) collective-permute-start(bf16[512,1024]{1,0:T(8,128)(2,1)} %convolution_convert_fusion.6), channel_id=1, source_target_pairs={{0,4},{1,5},{2,6},{3,7},{4,0},{5,1},{6,2},{7,3},{8,12},{9,13},{10,... | collective-permute-start | bytes 3145736 | tf_op jit(solution)/shard_map/ppermute | solution.py:53
  339.8 41.1 %collective-permute-start.32 = (bf16[512,1024]{1,0:T(8,128)(2,1)}, bf16[512,1024]{1,0:T(8,128)(2,1)}, u32[]{:S(2)}, u32[]{:S(2)}) collective-permute-start(bf16[512,1024]{1,0:T(8,128)(2,1)} %convolution_convert_fusion.10), channel_id=1, source_target_pairs={{0,4},{1,5},{2,6},{3,7},{4,0},{5,1},{6,2},{7,3},{8,12},{9,13},{10,... | collective-permute-start | bytes 3145736 | tf_op jit(solution)/shard_map/ppermute | solution.py:53
  378.4 86.1 %collective-permute-start.56 = (bf16[512,4608]{1,0:T(8,128)(2,1)}, bf16[512,4608]{1,0:T(8,128)(2,1)}, u32[]{:S(2)}, u32[]{:S(2)}) collective-permute-start(bf16[512,4608]{1,0:T(8,128)(2,1)} %convolution_convert_fusion.2), channel_id=1, source_target_pairs={{0,4},{1,5},{2,6},{3,7},{4,0},{5,1},{6,2},{7,3},{8,12},{9,13},{10,... | collective-permute-start | bytes 14155784 | tf_op jit(solution)/shard_map/ppermute | solution.py:53
  380.9 93.2 %collective-permute-start.50 = (bf16[512,4608]{1,0:T(8,128)(2,1)}, bf16[512,4608]{1,0:T(8,128)(2,1)}, u32[]{:S(2)}, u32[]{:S(2)}) collective-permute-start(bf16[512,4608]{1,0:T(8,128)(2,1)} %convolution_convert_fusion.4), channel_id=1, source_target_pairs={{0,4},{1,5},{2,6},{3,7},{4,0},{5,1},{6,2},{7,3},{8,12},{9,13},{10,... | collective-permute-start | bytes 14155784 | tf_op jit(solution)/shard_map/ppermute | solution.py:53
  472.1 56.6 %collective-permute-start.57 = (bf16[256,4608]{1,0:T(8,128)(2,1)}, bf16[256,4608]{1,0:T(8,128)(2,1)}, u32[]{:S(2)}, u32[]{:S(2)}) collective-permute-start(bf16[256,4608]{1,0:T(8,128)(2,1)} %slice.687), channel_id=1, source_target_pairs={{0,16},{1,17},{2,18},{3,19},{4,12},{5,13},{6,14},{7,15},{8,24},{9,... | collective-permute-start | bytes 7077896 | tf_op jit(solution)/shard_map/ppermute | solution.py:53
  482.2 89.0 %collective-permute-start.51 = (bf16[256,4608]{1,0:T(8,128)(2,1)}, bf16[256,4608]{1,0:T(8,128)(2,1)}, u32[]{:S(2)}, u32[]{:S(2)}) collective-permute-start(bf16[256,4608]{1,0:T(8,128)(2,1)} %slice.688), channel_id=1, source_target_pairs={{0,16},{1,17},{2,18},{3,19},{4,12},{5,13},{6,14},{7,15},{8,24},{9,... | collective-permute-start | bytes 7077896 | tf_op jit(solution)/shard_map/ppermute | solution.py:53
  488.3 86.9 %collective-permute-start.64 = (bf16[128,4608]{1,0:T(8,128)(2,1)}, bf16[128,4608]{1,0:T(8,128)(2,1)}, u32[]{:S(2)}, u32[]{:S(2)}) collective-permute-start(bf16[128,4608]{1,0:T(8,128)(2,1)} %slice.689), channel_id=1, source_target_pairs={{0,8},{1,9},{2,10},{3,11},{4,20},{5,21},{6,22},{7,23},{8,0},{9,1},... | collective-permute-start | bytes 3538952 | tf_op jit(solution)/shard_map/ppermute | solution.py:53
  531.1 49.7 %collective-permute-start.58 = (bf16[128,4608]{1,0:T(8,128)(2,1)S(1)}, bf16[128,4608]{1,0:T(8,128)(2,1)S(1)}, u32[]{:S(2)}, u32[]{:S(2)}) collective-permute-start(bf16[128,4608]{1,0:T(8,128)(2,1)S(1)} %slice.690), channel_id=1, source_target_pairs={{0,8},{1,9},{2,10},{3,11},{4,20},{5,21},{6,22},{7,23},{8,0},{9,1},... | collective-permute-start | bytes 3538952 | tf_op jit(solution)/shard_map/ppermute | solution.py:53
  582.0 36.0 %collective-permute-start.59 = (bf16[128,1152]{1,0:T(8,128)(2,1)}, bf16[128,1152]{1,0:T(8,128)(2,1)}, u32[]{:S(2)}, u32[]{:S(2)}) collective-permute-start(bf16[128,1152]{1,0:T(8,128)(2,1)} %get-tuple-element.109), channel_id=1, source_target_pairs={{3,0},{0,1},{1,2},{2,3},{7,4},{4,5},{5,6},{6,7},{11,8},{8,9},{9,10... | collective-permute-start | bytes 884744 | tf_op jit(solution)/shard_map/ppermute | solution.py:53
  589.9 35.6 %collective-permute-start.60 = (bf16[128,1152]{1,0:T(8,128)(2,1)}, bf16[128,1152]{1,0:T(8,128)(2,1)}, u32[]{:S(2)}, u32[]{:S(2)}) collective-permute-start(bf16[128,1152]{1,0:T(8,128)(2,1)} %get-tuple-element.111), channel_id=1, source_target_pairs={{2,0},{3,1},{0,2},{1,3},{6,4},{7,5},{4,6},{5,7},{10,8},{11,9},{8,1... | collective-permute-start | bytes 884744 | tf_op jit(solution)/shard_map/ppermute | solution.py:53
  (140 other events, 2325.9 us)

commit v2 on v1

v2 whole, which is shorter than its diff:
```python
import jax
import jax.numpy as jnp
from jax import lax
from jax.experimental import pallas as pl
from jax.experimental.pallas import tpu as pltpu
from jax.sharding import PartitionSpec as P

LEN = 1024
epsilon = 1e-05
AXES = ("dp", "tensor")
bf16 = jnp.bfloat16
f32 = jnp.float32
TOKEN_BLOCK = 512
INTERPRET = False


class Links:
    def __init__(self, dp, tensor):
        self.dp, self.tensor = dp, tensor
        self.bits = (dp // 2).bit_length() - 1
        assert dp == 2 << self.bits and self.bits >= 1
        self.devices = [(d, t) for d in range(dp) for t in range(tensor)]

    def at(self, d, t):
        return d * self.tensor + t

    def pairs(self, target):
        return [(self.at(d, t), self.at(*target(d, t))) for d, t in self.devices]

    def shift(self, k):
        return self.pairs(lambda d, t: (d, (t - k) % self.tensor))

    def bit(self, core, step):
        return step if core == 0 else self.bits - 1 - step

    def step(self, j):
        return self.pairs(lambda d, t: (d ^ (2 << self.bit(d % 2, j)), t))

    def flip(self, j):
        return self.pairs(lambda d, t: (d ^ (2 << j), t))

    def cores(self):
        return self.pairs(lambda d, t: (d ^ 1, t))

    def spread(self, p):
        return ((p << 1) | (p >> self.bits)) & (self.dp - 1)


def send(x, pairs):
    return lax.ppermute(x, AXES, pairs)


def dot(a, b, ca, cb):
    return lax.dot_general(a, b, (((ca,), (cb,)), ((), ())), preferred_element_type=f32)


def norm_rows(values):
    scale = lax.rsqrt(jnp.mean(values * values, axis=-1, keepdims=True) + epsilon)
    return (values * scale, scale)


def norm_back(grad_h, normed, scale, gain):
    grad_n = grad_h * gain
    inner = jnp.mean(grad_n * normed, axis=-1, keepdims=True)
    return scale * (grad_n - normed * inner)


def after(x, *others):
    return lax.optimization_barrier((x,) + others)[0]


def ffn_kernel(first_call, part, *refs):
    if first_call:
        h_ref, g_ref, *w_refs, dh_ref, ffn_ref, own0_ref, own1_ref, other_ref, acc_ref = refs
        dh_sum, ffn_sum = None, None
    else:
        h_ref, g_ref, *w_refs, dh_sum, ffn_sum, dh_ref, ffn_ref, own0_ref, own1_ref, other_ref, acc_ref = refs
    step = pl.program_id(0)
    both = 2 * part
    q = w_refs[0].shape[1]
    h, g = h_ref[...], g_ref[...]
    cut = [slice(i * q, (i + 1) * q) for i in range(4)]
    gate_up = sum(dot(w[:both], h[:, c], 1, 1) for w, c in zip(w_refs, cut))
    d_hidden = sum(dot(w[both:], g[:, c], 1, 1) for w, c in zip(w_refs, cut))
    gate, up = gate_up[:part], gate_up[part:]
    sigma = 1.0 / (1.0 + jnp.exp(-gate))
    silu = gate * sigma
    hidden = (silu * up).astype(bf16)
    d_gate = (d_hidden * up * sigma * (1.0 + gate * (1.0 - sigma))).astype(bf16)
    d_up = (d_hidden * silu).astype(bf16)
    d_both = jnp.concatenate([d_gate, d_up], axis=0)
    for w, c in zip(w_refs, cut):
        d_h = dot(d_both, w[:both], 0, 0)
        ffn = dot(hidden, w[both:], 0, 0)
        dh_ref[:, c] = d_h if first_call else dh_sum[:, c] + d_h
        ffn_ref[:, c] = ffn if first_call else ffn_sum[:, c] + ffn

    @pl.when(step == 0)
    def _():
        acc_ref[:both] = dot(d_both, h, 1, 0)
        acc_ref[both:] = dot(hidden, g, 1, 0)

    @pl.when(step > 0)
    def _():
        acc_ref[:both] += dot(d_both, h, 1, 0)
        acc_ref[both:] += dot(hidden, g, 1, 0)

    @pl.when(step == pl.num_programs(0) - 1)
    def _():
        own0_ref[...] = acc_ref[:, cut[0]].astype(bf16)
        own1_ref[...] = acc_ref[:, cut[1]].astype(bf16)
        other_ref[...] = acc_ref[:, 2 * q :].astype(bf16)


def ffn_chunk(h, g, weights, totals, token_block):
    tokens, D = h.shape
    n, q = weights[0].shape
    part = n // 3
    first_call = totals is None
    by_tokens = pl.BlockSpec((token_block, D), lambda i: (i, 0))
    whole = lambda w: pl.BlockSpec((n, w), lambda i: (0, 0))
    args = [h, g, *weights] + ([] if first_call else list(totals))
    specs = [by_tokens, by_tokens] + [whole(q)] * 4 + ([] if first_call else [by_tokens] * 2)

    def kernel(*refs):
        ffn_kernel(first_call, part, *refs)

    return pl.pallas_call(
        kernel,
        grid=(tokens // token_block,),
        in_specs=specs,
        out_specs=[
            by_tokens,
            by_tokens,
            whole(q),
            whole(q),
            whole(2 * q),
        ],
        out_shape=[
            jax.ShapeDtypeStruct((tokens, D), f32),
            jax.ShapeDtypeStruct((tokens, D), f32),
            jax.ShapeDtypeStruct((n, q), bf16),
            jax.ShapeDtypeStruct((n, q), bf16),
            jax.ShapeDtypeStruct((n, 2 * q), bf16),
        ],
        scratch_shapes=[pltpu.VMEM((n, D), f32)],
        compiler_params=pltpu.CompilerParams(
            dimension_semantics=("arbitrary",), vmem_limit_bytes=52 * 1024 * 1024
        ),
        cost_estimate=pl.CostEstimate(
            flops=20 * tokens * D * part, bytes_accessed=12 * n * q * 2, transcendentals=tokens * part
        ),
        interpret=INTERPRET,
    )(*args)


def make_body(links):
    dp, T = links.dp, links.tensor

    def body(x_in, in_w, out_w, gate_w, up_w, down_w, conv_w, gain1, gain2, d_out):
        rows, D = x_in.shape
        block = D // dp
        half = D // 2
        chan = in_w.shape[2]
        C = chan * T
        part = gate_w.shape[1] // 2
        per_seq = LEN // rows
        me_dp = lax.axis_index("dp")
        me_t = lax.axis_index("tensor")
        me_x = (me_dp // 2) % 2
        core = me_dp % 2
        groups = dp // 2
        canonical = [
            [sum(((q >> links.bit(c, j)) & 1) << j for j in range(links.bits)) for q in range(groups)] for c in (0, 1)
        ]
        walked = [[order.index(p) for p in range(groups)] for order in canonical]

        def by_core(blocks, order):
            a, b = order
            return [blocks[i] if i == j else jnp.where(core == 0, blocks[i], blocks[j]) for i, j in zip(a, b)]

        def walk_back(own, got):
            x = own.astype(f32) + got.astype(f32)
            blocks = by_core([x[i * block : (i + 1) * block] for i in range(groups)], walked)
            for j in reversed(range(links.bits)):
                n = len(blocks) // 2
                sent = send(jnp.concatenate(blocks[n:], axis=0).astype(bf16), links.step(j)).astype(f32)
                blocks = [blocks[i] + sent[i * block : (i + 1) * block] for i in range(n)]
            return blocks[0]

        def shift_back(k, x):
            return send(x.astype(bf16), [(b, a) for a, b in links.shift(k)])

        def swap(v):
            parts = [v[:, (p ^ 1) * block : ((p ^ 1) + 1) * block] for p in range(dp)]
            return jnp.concatenate(parts, axis=1)

        mine = me_dp ^ jnp.asarray([links.spread(p) for p in range(dp)], jnp.int32)
        source = (mine[:, None] * block + jnp.arange(block)[None, :]).reshape(D)
        place = (jnp.arange(D)[:, None] == source[None, :]).astype(bf16)

        def arrange(v):
            return dot(v, place, 1, 0).astype(bf16)

        def restore(v):
            return dot(v, place, 1, 1).astype(bf16)

        def restore_rows(v):
            return jnp.sum(
                jnp.where((mine[None, :] == jnp.arange(dp)[:, None])[:, :, None], v.reshape(1, dp, block), 0.0), axis=1
            ).reshape(D)

        in_own = in_w.reshape(block, 3 * chan)
        in_k = [in_own] + [send(in_own, links.shift(k)) for k in range(1, T)]
        stack = jnp.concatenate([w.reshape(2, part, block) for w in (gate_w.T, up_w.T, down_w)], axis=1)
        ffn_keep = jnp.where(me_x == 0, stack[0], stack[1])
        ffn_give = jnp.where(me_x == 0, stack[1], stack[0])
        ffn_own = jnp.concatenate([ffn_keep, send(ffn_give, links.flip(0))], axis=1)

        own = [ffn_own]
        near = [[] for _ in range(T)]

        def shift_chunk(*waits):
            if len(own) < T:
                own.append(send(after(own[-1], *waits), links.shift(1)))

        def exchange(k, *waits):
            if k < T:
                x = after(own[k], *waits)
                for j in range(1, links.bits):
                    got = send(x, links.flip(j))
                    near[k] = [x, got]
                    if j < links.bits - 1:
                        x = jnp.concatenate(near[k], axis=1)

        def walk_first(x):
            return [x, send(x, links.step(0))]

        def walk_rest(blocks, *waits):
            for j in range(1, links.bits):
                whole = jnp.concatenate(blocks, axis=0)
                if j == 1:
                    whole = after(whole, *waits)
                got = send(whole, links.step(j))
                blocks = blocks + [got[i * block : (i + 1) * block] for i in range(len(blocks))]
            return blocks

        in_cols = jnp.concatenate([w[:, i * chan : (i + 1) * chan] for i in range(3) for w in in_k], axis=1)
        in_cols = after(in_cols, ffn_own)
        in_first = walk_first(in_cols)
        out_own = after(out_w.T, in_cols)
        out_k = [out_own] + [send(out_own, links.shift(k)) for k in range(1, T)]
        out_cols = jnp.concatenate(out_k, axis=1)
        slot2 = [in_first[1], out_cols]
        in_walked = walk_rest(in_first, *slot2)
        out_first = walk_first(after(out_cols, *slot2))
        shift_chunk(*slot2)
        slot3 = [in_walked[-1], own[-1], out_first[1]]
        in0 = after(jnp.concatenate(by_core(in_walked, canonical), axis=0), *slot3)
        in1 = send(in0, links.cores())
        out_walked = walk_rest(out_first, *slot3)
        shift_chunk(*slot3)
        exchange(1, *slot3)
        out0 = jnp.concatenate(by_core(out_walked, canonical), axis=0)
        out1 = send(out0, links.cores())

        tokens = arrange(x_in).astype(f32)
        cot16 = arrange(d_out)
        partner_cot = send(after(swap(cot16), *slot3), links.flip(0))
        gains = arrange(jnp.stack([gain1, gain2])).astype(f32)
        gain_one, gain_two = gains[0], gains[1]
        turned = jnp.concatenate([conv_w, conv_w], axis=1)
        kernel = lax.dynamic_slice_in_dim(turned, me_t * chan, C, 1).astype(f32)

        def split(a, axis=1):
            return lax.slice_in_dim(a, 0, half, axis=axis), lax.slice_in_dim(a, half, D, axis=axis)

        normed_one, scale_one = norm_rows(tokens)
        first = (normed_one * gain_one).astype(bf16)
        f0, f1 = split(first)
        projected = dot(f0, in0, 1, 0) + dot(f1, in1, 1, 0)
        b_part, c_part, x_part = projected[:, :C], projected[:, C : 2 * C], projected[:, 2 * C :]
        mixed_in = b_part * x_part
        follows = [(links.at(d, t), links.at(d, t + 1)) for d, t in links.devices if (t + 1) % per_seq]
        no_rows = jnp.zeros((2, C), f32)
        before = send(jnp.roll(mixed_in[rows - 2 :], -chan, axis=1), follows) if follows else no_rows
        lead = jnp.concatenate([before, mixed_in[: rows - 1]], axis=0)
        back_one = lead[1:]
        back_two = lead[:rows]
        conv_out = kernel[2] * mixed_in + kernel[1] * back_one + kernel[0] * back_two
        branch = (c_part * conv_out).astype(bf16)
        slot4 = [out_walked[-1], own[-1], partner_cot] + near[1 % T]
        branch = after(branch, *slot4)
        exchange(2, branch)
        shift_chunk(branch)
        resid = tokens + jnp.concatenate([dot(branch, out0, 1, 1), dot(branch, out1, 1, 1)], axis=1)
        normed_two, scale_two = norm_rows(resid)
        second = (normed_two * gain_two).astype(bf16)
        cot_all = jnp.concatenate([partner_cot, cot16], axis=0)
        second_all = jnp.concatenate([send(swap(second), links.flip(0)), second], axis=0)

        def core_sum(k, sums):
            own0, own1, other = sums
            got = send(other, links.cores()).astype(f32)
            return own0.astype(f32) + got[:, : half // 2], (own1.astype(f32) + got[:, half // 2 :]).astype(bf16)

        def group_sum(kept, sent):
            x = kept + send(sent, links.flip(links.bits - 1)).astype(f32)
            for j in reversed(range(1, links.bits - 1)):
                n = x.shape[1] // 2
                x = x[:, :n] + send(x[:, n:].astype(bf16), links.flip(j)).astype(f32)
            return x

        def other_core(k):
            return near[k] + [send(x, links.cores()) for x in near[k]]

        turn = list(range(1, T)) + [0]
        totals = None
        sums, cored, grouped, shifted = {}, {}, {}, {}
        weights = {}
        if T == 1:
            exchange(0)
        weights[turn[0]] = other_core(turn[0])
        slot = weights[turn[0]] + [x for k in turn[:2] for x in near[k]] + own
        for i, k in enumerate(turn):
            h_in = after(second_all, *slot)
            slot = []
            if i + 2 < T:
                exchange(turn[i + 2], h_in)
                slot += near[turn[i + 2]]
            if i + 1 < T:
                weights[turn[i + 1]] = other_core(turn[i + 1])
                slot += weights[turn[i + 1]]
            if i >= 1:
                cored[i - 1] = core_sum(turn[i - 1], sums[i - 1])
                slot += cored[i - 1]
            if i >= 2:
                grouped[i - 2] = group_sum(*cored[i - 2])
                slot.append(grouped[i - 2])
            if i >= 3:
                shifted[i - 3] = shift_back(turn[i - 3], grouped[i - 3])
                slot.append(shifted[i - 3])
            d_h, ffn, *sums[i] = ffn_chunk(h_in, cot_all, weights[k], totals, min(TOKEN_BLOCK, 2 * rows))
            totals = (d_h, ffn)

        theirs = send(swap(d_h[:rows].astype(bf16)), links.flip(0))
        ready = after(d_h[:8], *slot)
        cored[T - 1] = core_sum(turn[T - 1], sums[T - 1])
        if T > 1:
            grouped[T - 2] = group_sum(cored[T - 2][0], after(cored[T - 2][1], ready))
        if T > 2:
            shifted[T - 3] = shift_back(turn[T - 3], after(grouped[T - 3], ready))
        theirs = after(theirs, *cored[T - 1], ready)
        d_second = d_h[rows:] + theirs.astype(f32)
        ffn_sent = send(after(swap(ffn[:rows].astype(bf16)), theirs), links.flip(0))
        ffn_theirs = ffn_sent.astype(f32)

        gain_two_part = jnp.sum(d_second * normed_two, axis=0)
        d_resid = cot16.astype(f32) + norm_back(d_second, normed_two, scale_two, gain_two)
        d_mixed = d_resid.astype(bf16)
        m0, m1 = split(d_mixed)
        d_branch = dot(m0, out0, 1, 0) + dot(m1, out1, 1, 0)
        d_conv = d_branch * c_part
        d_c = d_branch * conv_out
        leads = [(b, a) for a, b in follows]
        edge = send(jnp.roll(d_conv[:2], chan, axis=1), leads) if leads else no_rows
        d_c = d_c.astype(bf16)
        first_other = jnp.concatenate([dot(m1, branch, 0, 0), dot(f1, d_c, 0, 0)], axis=1).astype(bf16)
        first_got = send(first_other, links.cores())
        first_own = jnp.concatenate([dot(m0, branch, 0, 0), dot(f0, d_c, 0, 0)], axis=1).astype(bf16)
        edge = after(edge, first_own)
        trail = jnp.concatenate([d_conv[1:], edge], axis=0)
        d_mixin = kernel[2] * d_conv + kernel[1] * trail[:rows] + kernel[0] * trail[1:]
        taps = [jnp.sum(d_conv * v, axis=0) for v in (back_two, back_one, mixed_in)]
        d_bx = jnp.concatenate([(d_mixin * v).astype(bf16) for v in (x_part, b_part)], axis=1)
        d_bx = after(d_bx, first_got, *[grouped[i] for i in grouped], *[shifted[i] for i in shifted])
        last_other = dot(f1, d_bx, 0, 0).astype(bf16)
        last_got = send(last_other, links.cores())
        last_own = dot(f0, d_bx, 0, 0).astype(bf16)
        grouped[T - 1] = group_sum(cored[T - 1][0], after(cored[T - 1][1], d_bx))
        if T > 1:
            shifted[T - 2] = shift_back(turn[T - 2], after(grouped[T - 2], d_bx))

        def pieces(v, parts):
            take = lambda i, k: v[:, i * C + k * chan : i * C + (k + 1) * chan]
            return [jnp.concatenate([take(i, k) for i in range(parts)], axis=1) for k in range(T)]

        def all_shifts(blocks):
            return blocks[0] + sum(shift_back(k, blocks[k]).astype(f32) for k in range(1, T))

        first_sum = all_shifts(pieces(walk_back(first_own, first_got), 2))
        last_sum = all_shifts(pieces(walk_back(last_own, last_got), 2))
        grad_out = first_sum[:, :chan]
        grad_in = jnp.stack([last_sum[:, :chan], first_sum[:, chan:], last_sum[:, chan:]], axis=1)

        d_proj = after(jnp.concatenate([d_bx[:, :C], d_c, d_bx[:, C:]], axis=1), last_got)
        d_first = jnp.concatenate([dot(d_proj, in0, 1, 1), dot(d_proj, in1, 1, 1)], axis=1)
        gain_one_part = jnp.sum(d_first * normed_one, axis=0)
        d_x = restore((d_resid + norm_back(d_first, normed_one, scale_one, gain_one)).astype(bf16))
        block_out = restore((resid + ffn[rows:] + ffn_theirs).astype(bf16))

        total = grouped[T - 1] + sum(shifted[i].astype(f32) for i in shifted)
        ours, yours = total[:, :block], send(total[:, block:].astype(bf16), links.flip(0)).astype(f32)
        low = jnp.where(me_x == 0, ours, yours)
        high = jnp.where(me_x == 0, yours, ours)
        grads = [
            jnp.concatenate([low[i * part : (i + 1) * part], high[i * part : (i + 1) * part]], axis=0) for i in range(3)
        ]

        taps = jnp.stack(taps)
        taps = lax.dynamic_slice_in_dim(jnp.concatenate([taps, taps], axis=1), C - me_t * chan, C, 1)
        small = jnp.concatenate([taps, restore_rows(gain_one_part)[None], restore_rows(gain_two_part)[None]], axis=0)
        small = small + send(small, links.cores())
        for j in range(links.bits):
            small = small + send(small, links.flip(j))
        k = 1
        while k < T:
            small = small + send(small, links.pairs(lambda d, t: (d, t ^ k)))
            k *= 2
        return (
            block_out,
            d_x,
            grad_in,
            grad_out.T,
            grads[0].T,
            grads[1].T,
            grads[2],
            small[:3],
            small[3],
            small[4],
        )

    return body


def solution(mesh):
    links = Links(mesh.shape["dp"], mesh.shape["tensor"])
    in_specs = (
        P(("dp", "tensor"), None),
        P("dp", None, "tensor"),
        P("tensor", "dp"),
        P("dp", "tensor"),
        P("dp", "tensor"),
        P("tensor", "dp"),
        P(),
        P(),
        P(),
        P(("dp", "tensor"), None),
    )
    out_specs = (
        P(("dp", "tensor"), None),
        P(("dp", "tensor"), None),
        P("dp", None, "tensor"),
        P("tensor", "dp"),
        P("dp", "tensor"),
        P("dp", "tensor"),
        P("tensor", "dp"),
        P(),
        P(),
        P(),
    )
    return jax.shard_map(
        make_body(links), mesh=mesh, in_specs=in_specs, out_specs=out_specs, check_vma=False
    )
```

time: 640 us -> 449 us (0.70)
  the two profiles are of different devices: /device:TPU:0 before, /device:TPU:15 now
where the time goes in v2:
time: 449 us; the launch traced here: 440 us
  waiting for transfers between devices  172 us (38%)
  Pallas kernels  80.1 us (18%)
  starting transfers between devices  67.5 us (15%)
  other arithmetic  53.9 us (12%)
  matrix products  38.6 us (9%)
  local copies, waits for them, and re-layouts  25.5 us (6%)
    ppermute x63, waiting for transfers between devices, send(): return lax.ppermute(x, AXES, pairs)  172 us
    pallas_call x4, Pallas kernels, ffn_chunk(): pl.pallas_call(kernel, grid=(tokens // token_block,), in_specs=specs, out...  80.1 us
    ppermute x63, starting transfers between devices, send(): return lax.ppermute(x, AXES, pairs)  67.5 us
    dot_general x19, matrix products, dot(): lax.dot_general(a, b, (((ca,), (cb,)), ((), ())), preferred_element_type=...  38.6 us
    unnamed x172, local copies, waits for them, and re-layouts  19.3 us
  transfers between devices with their start and end apart: 63, of which 24 were waited for; matrix products, arithmetic and copies ran while one was open for 22% of the time, Pallas kernels for 18%

profile of v2, /device:TPU:15, one launch (start us, length us, event | category | flops | bytes accessed | tf_op | source)
XLA Modules:
  0.0 440.5 jit_solution(579613059570805056)
XLA Ops:
  10.4 6.3 %collective-permute-done.1 = bf16[128,768]{0,1:T(8,128)(2,1)S(1)} collective-permute-done((bf16[128,768]{0,1:T(8,128)(2,1)S(1)}, bf16[128,768]{0,1:T(8,128)(2,1)S(1)}, u32[]{:S(2)}, u32[]{:S(2)}) %collective-permute-start.1) | collective-permute-done | bytes 196640 | tf_op jit(solution)/shard_map/ppermute | solution.py:50
  16.7 4.2 collective-permute-done.2
  39.2 18.9 %collective-permute-done.8 = bf16[256,3072]{0,1:T(8,128)(2,1)} collective-permute-done((bf16[256,3072]{0,1:T(8,128)(2,1)}, bf16[256,3072]{0,1:T(8,128)(2,1)}, u32[]{:S(2)}, u32[]{:S(2)}) %collective-permute-start.8) | collective-permute-done | bytes 1572896 | tf_op jit(solution)/shard_map/ppermute | solution.py:50
  70.7 5.9 %collective-permute-done.13 = bf16[256,1024]{0,1:T(8,128)(2,1)S(1)} collective-permute-done((bf16[256,1024]{0,1:T(8,128)(2,1)S(1)}, bf16[256,1024]{0,1:T(8,128)(2,1)S(1)}, u32[]{:S(2)}, u32[]{:S(2)}) %collective-permute-start.13) | collective-permute-done | bytes 524320 | tf_op jit(solution)/shard_map/ppermute | solution.py:50
  76.9 6.5 %collective-permute-start.17 = (bf16[512,1024]{0,1:T(8,128)(2,1)S(1)}, bf16[512,1024]{0,1:T(8,128)(2,1)S(1)}, u32[]{:S(2)}, u32[]{:S(2)}) collective-permute-start(bf16[512,1024]{0,1:T(8,128)(2,1)S(1)} %pad_maximum_fusion.11), channel_id=1, source_target_pairs={{0,4},{1,5},{2,6},{3,7},{4,0},{5,1},{6,2},{7,3},{8,12},{9,13},{10,... | collective-permute-start | bytes 3145736 | tf_op jit(solution)/shard_map/ppermute | solution.py:50
  83.3 3.7 fusion.51
  87.1 3.8 convolution_add_fusion
  106.0 16.8 %collective-permute-done.22.refs_3_ = bf16[1728,256]{1,0:T(8,128)(2,1)S(1)} collective-permute-done((bf16[1728,256]{1,0:T(8,128)(2,1)S(1)}, bf16[1728,256]{1,0:T(8,128)(2,1)S(1)}, u32[]{:S(2)}, u32[]{:S(2)}) %collective-permute-start.22) | collective-permute-done | bytes 884768 | tf_op jit(solution)/shard_map/ppermute | solution.py:50
  130.7 18.7 %shard_map.186 = (f32[1024,1024]{1,0:T(8,128)}, f32[1024,1024]{1,0:T(8,128)}, bf16[1728,256]{1,0:T(8,128)(2,1)S(1)}, bf16[1728,256]{1,0:T(8,128)(2,1)S(1)}, bf16[1728,512]{1,0:T(8,128)(2,1)}) custom-call(bf16[1024,1024]{1,0:T(8,128)(2,1)} %pad_maximum_fusion.4.refs_0_, bf16[1024,1024]{1,0:T(8,128)(2,1)} %pad_maximum_fusion.5.refs_1_, ...), custom_call_target="tpu_custom_call" | custom-call | flops 12079595520 | bytes 10616832 | tf_op jit(solution)/shard_map/pallas_call | solution.py:128
  151.3 20.4 %shard_map.187 = (f32[1024,1024]{1,0:T(8,128)}, f32[1024,1024]{1,0:T(8,128)}, bf16[1728,256]{1,0:T(8,128)(2,1)S(1)}, bf16[1728,256]{1,0:T(8,128)(2,1)S(1)}, bf16[1728,512]{1,0:T(8,128)(2,1)}) custom-call(bf16[1024,1024]{1,0:T(8,128)(2,1)} %pad_maximum_fusion.4.refs_0_, bf16[1024,1024]{1,0:T(8,128)(2,1)} %pad_maximum_fusion.5.refs_1_, ...), custom_call_target="tpu_custom_call" | custom-call | flops 12079595520 | bytes 10616832 | tf_op jit(solution)/shard_map/pallas_call | solution.py:128
  177.5 19.4 %collective-permute-done.31 = bf16[1728,256]{1,0:T(8,128)(2,1)} collective-permute-done((bf16[1728,256]{1,0:T(8,128)(2,1)}, bf16[1728,256]{1,0:T(8,128)(2,1)}, u32[]{:S(2)}, u32[]{:S(2)}) %collective-permute-start.31) | collective-permute-done | bytes 884768 | tf_op jit(solution)/shard_map/ppermute | solution.py:50
  204.3 20.4 %shard_map.188 = (f32[1024,1024]{1,0:T(8,128)}, f32[1024,1024]{1,0:T(8,128)}, bf16[1728,256]{1,0:T(8,128)(2,1)S(1)}, bf16[1728,256]{1,0:T(8,128)(2,1)S(1)}, bf16[1728,512]{1,0:T(8,128)(2,1)}) custom-call(bf16[1024,1024]{1,0:T(8,128)(2,1)} %pad_maximum_fusion.4.refs_0_, bf16[1024,1024]{1,0:T(8,128)(2,1)} %pad_maximum_fusion.5.refs_1_, ...), custom_call_target="tpu_custom_call" | custom-call | flops 12079595520 | bytes 10616832 | tf_op jit(solution)/shard_map/pallas_call | solution.py:128
  228.3 20.7 %shard_map.189 = (f32[1024,1024]{1,0:T(8,128)}, f32[1024,1024]{1,0:T(8,128)}, bf16[1728,256]{1,0:T(8,128)(2,1)S(1)}, bf16[1728,256]{1,0:T(8,128)(2,1)S(1)}, bf16[1728,512]{1,0:T(8,128)(2,1)}) custom-call(bf16[1024,1024]{1,0:T(8,128)(2,1)} %pad_maximum_fusion.4.refs_0_, bf16[1024,1024]{1,0:T(8,128)(2,1)} %pad_maximum_fusion.5.refs_1_, ...), custom_call_target="tpu_custom_call" | custom-call | flops 12079595520 | bytes 10616832 | tf_op jit(solution)/shard_map/pallas_call | solution.py:128
  266.4 11.3 %collective-permute-done.34 = bf16[512,1024]{1,0:T(8,128)(2,1)S(1)} collective-permute-done((bf16[512,1024]{1,0:T(8,128)(2,1)S(1)}, bf16[512,1024]{1,0:T(8,128)(2,1)S(1)}, u32[]{:S(2)}, u32[]{:S(2)}) %collective-permute-start.34) | collective-permute-done | bytes 1048608 | tf_op jit(solution)/shard_map/ppermute | solution.py:50
  296.6 18.3 %collective-permute-done.39 = bf16[512,1024]{1,0:T(8,128)(2,1)} collective-permute-done((bf16[512,1024]{1,0:T(8,128)(2,1)}, bf16[512,1024]{1,0:T(8,128)(2,1)}, u32[]{:S(2)}, u32[]{:S(2)}) %collective-permute-start.39) | collective-permute-done | bytes 1048608 | tf_op jit(solution)/shard_map/ppermute | solution.py:50
  314.9 3.6 fusion.34
  326.0 17.5 %collective-permute-done.55 = bf16[1728,256]{1,0:T(8,128)(2,1)S(1)} collective-permute-done((bf16[1728,256]{1,0:T(8,128)(2,1)S(1)}, bf16[1728,256]{1,0:T(8,128)(2,1)S(1)}, u32[]{:S(2)}, u32[]{:S(2)}) %collective-permute-start.55) | collective-permute-done | bytes 884768 | tf_op jit(solution)/shard_map/ppermute | solution.py:50
  348.3 7.7 %collective-permute-done.57 = bf16[1728,128]{1,0:T(8,128)(2,1)S(1)} collective-permute-done((bf16[1728,128]{1,0:T(8,128)(2,1)S(1)}, bf16[1728,128]{1,0:T(8,128)(2,1)S(1)}, u32[]{:S(2)}, u32[]{:S(2)}) %collective-permute-start.57) | collective-permute-done | bytes 442400 | tf_op jit(solution)/shard_map/ppermute | solution.py:50
  368.4 3.7 fusion.87
  372.1 4.1 fusion.88
  377.2 8.0 %collective-permute-start.58 = (f32[5,1024]{1,0:T(8,128)S(1)}, f32[5,1024]{1,0:T(8,128)S(1)}, u32[]{:S(2)}, u32[]{:S(2)}) collective-permute-start(f32[5,1024]{1,0:T(8,128)S(1)} %pad_maximum_fusion.25), channel_id=1, source_target_pairs={{0,4},{1,5},{2,6},{3,7},{4,0},{5,1},{6,2},{7,3},{8,12},{9,13},{10,... | collective-permute-start | bytes 61448 | tf_op jit(solution)/shard_map/ppermute | solution.py:50
  391.8 13.0 %collective-permute-done.59 = f32[5,1024]{1,0:T(8,128)S(1)} collective-permute-done((f32[5,1024]{1,0:T(8,128)S(1)}, f32[5,1024]{1,0:T(8,128)S(1)}, u32[]{:S(2)}, u32[]{:S(2)}) %collective-permute-start.59) | collective-permute-done | bytes 20512 | tf_op jit(solution)/shard_map/ppermute | solution.py:50
  419.3 3.8 collective-permute-done.46
  429.1 6.9 %collective-permute-done.48 = bf16[128,512]{1,0:T(8,128)(2,1)S(1)} collective-permute-done((bf16[128,512]{1,0:T(8,128)(2,1)S(1)}, bf16[128,512]{1,0:T(8,128)(2,1)S(1)}, u32[]{:S(2)}, u32[]{:S(2)}) %collective-permute-start.48) | collective-permute-done | bytes 131104 | tf_op jit(solution)/shard_map/ppermute | solution.py:50
  (406 shorter events, 174.4 us)
Async XLA Ops:
  68.8 29.8 %collective-permute-start.14 = (bf16[1728,256]{1,0:T(8,128)(2,1)S(1)}, bf16[1728,256]{1,0:T(8,128)(2,1)S(1)}, u32[]{:S(2)}, u32[]{:S(2)}) collective-permute-start(bf16[1728,256]{1,0:T(8,128)(2,1)S(1)} %copy-done.51), channel_id=1, source_target_pairs={{0,3},{1,0},{2,1},{3,2},{4,7},{5,4},{6,5},{7,6},{8,11},{9,8},{10,9... | collective-permute-start | bytes 2654216 | tf_op jit(solution)/shard_map/ppermute | solution.py:50
  69.5 29.1 %collective-permute-start.16 = (bf16[1728,256]{1,0:T(8,128)(2,1)S(1)}, bf16[1728,256]{1,0:T(8,128)(2,1)S(1)}, u32[]{:S(2)}, u32[]{:S(2)}) collective-permute-start(bf16[1728,256]{1,0:T(8,128)(2,1)S(1)} %copy-done.51), channel_id=1, source_target_pairs={{0,16},{1,17},{2,18},{3,19},{4,20},{5,21},{6,22},{7,23},{8,24},{9,... | collective-permute-start | bytes 2654216 | tf_op jit(solution)/shard_map/ppermute | solution.py:50
  69.8 28.9 %collective-permute-start.15 = (bf16[512,1024]{1,0:T(8,128)(2,1)S(1)}, bf16[512,1024]{1,0:T(8,128)(2,1)S(1)}, u32[]{:S(2)}, u32[]{:S(2)}) collective-permute-start(bf16[512,1024]{1,0:T(8,128)(2,1)S(1)} %slice_dynamic-update-slice_fusion.24), channel_id=1, source_target_pairs={{0,8},{1,9},{2,10},{3,11},{4,12},{5,13},{6,14},{7,15},{8,0},{9,1},... | collective-permute-start | bytes 3145736 | tf_op jit(solution)/shard_map/ppermute | solution.py:50
  102.3 23.9 %collective-permute-start.18 = (bf16[512,1024]{1,0:T(8,128)(2,1)S(1)}, bf16[512,1024]{1,0:T(8,128)(2,1)S(1)}, u32[]{:S(2)}, u32[]{:S(2)}) collective-permute-start(bf16[512,1024]{1,0:T(8,128)(2,1)S(1)} %slice_dynamic-update-slice_fusion.16), channel_id=1, source_target_pairs={{0,8},{1,9},{2,10},{3,11},{4,12},{5,13},{6,14},{7,15},{8,0},{9,1},... | collective-permute-start | bytes 3145736 | tf_op jit(solution)/shard_map/ppermute | solution.py:50
  102.9 26.5 %collective-permute-start.20 = (bf16[1728,256]{1,0:T(8,128)(2,1)S(1)}, bf16[1728,256]{1,0:T(8,128)(2,1)S(1)}, u32[]{:S(2)}, u32[]{:S(2)}) collective-permute-start(bf16[1728,256]{1,0:T(8,128)(2,1)S(1)} %copy-done.51), channel_id=1, source_target_pairs={{0,4},{1,5},{2,6},{3,7},{4,0},{5,1},{6,2},{7,3},{8,12},{9,13},{10,... | collective-permute-start | bytes 2654216 | tf_op jit(solution)/shard_map/ppermute | solution.py:50
  104.3 25.1 %collective-permute-start.21 = (bf16[1728,256]{1,0:T(8,128)(2,1)S(1)}, bf16[1728,256]{1,0:T(8,128)(2,1)S(1)}, u32[]{:S(2)}, u32[]{:S(2)}) collective-permute-start(bf16[1728,256]{1,0:T(8,128)(2,1)S(1)} %collective-permute-done.16.refs_3_), channel_id=1, source_target_pairs={{0,4},{1,5},{2,6},{3,7},{4,0},{5,1},{6,2},{7,3},{8,12},{9,13},{10,... | collective-permute-start | bytes 2654216 | tf_op jit(solution)/shard_map/ppermute | solution.py:50
  104.3 25.1 %collective-permute-start.19 = (bf16[1728,256]{1,0:T(8,128)(2,1)S(1)}, bf16[1728,256]{1,0:T(8,128)(2,1)}, u32[]{:S(2)}, u32[]{:S(2)}) collective-permute-start(bf16[1728,256]{1,0:T(8,128)(2,1)S(1)} %collective-permute-done.14.refs_2_), channel_id=1, source_target_pairs={{0,3},{1,0},{2,1},{3,2},{4,7},{5,4},{6,5},{7,6},{8,11},{9,8},{10,9... | collective-permute-start | bytes 2654216 | tf_op jit(solution)/shard_map/ppermute | solution.py:50
  122.8 26.6 %collective-permute-start.24 = (bf16[1728,256]{1,0:T(8,128)(2,1)S(1)}, bf16[1728,256]{1,0:T(8,128)(2,1)S(1)}, u32[]{:S(2)}, u32[]{:S(2)}) collective-permute-start(bf16[1728,256]{1,0:T(8,128)(2,1)S(1)} %collective-permute-done.14.refs_2_), channel_id=1, source_target_pairs={{0,4},{1,5},{2,6},{3,7},{4,0},{5,1},{6,2},{7,3},{8,12},{9,13},{10,... | collective-permute-start | bytes 2654216 | tf_op jit(solution)/shard_map/ppermute | solution.py:50
  151.1 26.0 %collective-permute-start.26 = (bf16[1728,256]{1,0:T(8,128)(2,1)}, bf16[1728,256]{1,0:T(8,128)(2,1)}, u32[]{:S(2)}, u32[]{:S(2)}) collective-permute-start(bf16[1728,256]{1,0:T(8,128)(2,1)} %pad_maximum_fusion.15.refs_2_), channel_id=1, source_target_pairs={{0,16},{1,17},{2,18},{3,19},{4,20},{5,21},{6,22},{7,23},{8,24},{9,... | collective-permute-start | bytes 2654216 | tf_op jit(solution)/shard_map/ppermute | solution.py:50
  171.7 29.0 %collective-permute-start.29 = (bf16[1728,512]{1,0:T(8,128)(2,1)}, bf16[1728,512]{1,0:T(8,128)(2,1)}, u32[]{:S(2)}, u32[]{:S(2)}) collective-permute-start(bf16[1728,512]{1,0:T(8,128)(2,1)} %get-tuple-element.75), channel_id=1, source_target_pairs={{0,4},{1,5},{2,6},{3,7},{4,0},{5,1},{6,2},{7,3},{8,12},{9,13},{10,... | collective-permute-start | bytes 5308424 | tf_op jit(solution)/shard_map/ppermute | solution.py:50
  176.6 24.1 %collective-permute-start.32 = (bf16[1728,256]{1,0:T(8,128)(2,1)}, bf16[1728,256]{1,0:T(8,128)(2,1)}, u32[]{:S(2)}, u32[]{:S(2)}) collective-permute-start(bf16[1728,256]{1,0:T(8,128)(2,1)} %collective-permute-done.19.refs_2_), channel_id=1, source_target_pairs={{0,4},{1,5},{2,6},{3,7},{4,0},{5,1},{6,2},{7,3},{8,12},{9,13},{10,... | collective-permute-start | bytes 2654216 | tf_op jit(solution)/shard_map/ppermute | solution.py:50
  177.1 49.9 %collective-permute-start.27 = (bf16[1728,256]{1,0:T(8,128)(2,1)}, bf16[1728,256]{1,0:T(8,128)(2,1)S(1)}, u32[]{:S(2)}, u32[]{:S(2)}) collective-permute-start(bf16[1728,256]{1,0:T(8,128)(2,1)} %pad_maximum_fusion.15.refs_2_), channel_id=1, source_target_pairs={{0,4},{1,5},{2,6},{3,7},{4,0},{5,1},{6,2},{7,3},{8,12},{9,13},{10,... | collective-permute-start | bytes 2654216 | tf_op jit(solution)/shard_map/ppermute | solution.py:50
  197.0 30.1 %collective-permute-start.28 = (bf16[1728,256]{1,0:T(8,128)(2,1)}, bf16[1728,256]{1,0:T(8,128)(2,1)S(1)}, u32[]{:S(2)}, u32[]{:S(2)}) collective-permute-start(bf16[1728,256]{1,0:T(8,128)(2,1)} %collective-permute-done.26.refs_3_), channel_id=1, source_target_pairs={{0,4},{1,5},{2,6},{3,7},{4,0},{5,1},{6,2},{7,3},{8,12},{9,13},{10,... | collective-permute-start | bytes 2654216 | tf_op jit(solution)/shard_map/ppermute | solution.py:50
  224.6 34.4 %collective-permute-start.36 = (bf16[1728,512]{1,0:T(8,128)(2,1)}, bf16[1728,512]{1,0:T(8,128)(2,1)}, u32[]{:S(2)}, u32[]{:S(2)}) collective-permute-start(bf16[1728,512]{1,0:T(8,128)(2,1)} %get-tuple-element.92), channel_id=1, source_target_pairs={{0,4},{1,5},{2,6},{3,7},{4,0},{5,1},{6,2},{7,3},{8,12},{9,13},{10,... | collective-permute-start | bytes 5308424 | tf_op jit(solution)/shard_map/ppermute | solution.py:50
  225.0 37.3 %collective-permute-start.38 = (bf16[1728,256]{1,0:T(8,128)(2,1)}, bf16[1728,256]{1,0:T(8,128)(2,1)S(1)}, u32[]{:S(2)}, u32[]{:S(2)}) collective-permute-start(bf16[1728,256]{1,0:T(8,128)(2,1)} %convert_add_fusion.5), channel_id=1, source_target_pairs={{3,0},{0,1},{1,2},{2,3},{7,4},{4,5},{5,6},{6,7},{11,8},{8,9},{9,10... | collective-permute-start | bytes 2654216 | tf_op jit(solution)/shard_map/ppermute | solution.py:50
  252.7 24.9 %collective-permute-start.34 = (bf16[512,1024]{1,0:T(8,128)(2,1)S(1)}, bf16[512,1024]{1,0:T(8,128)(2,1)S(1)}, u32[]{:S(2)}, u32[]{:S(2)}) collective-permute-start(bf16[512,1024]{1,0:T(8,128)(2,1)S(1)} %slice_dynamic-update-slice_fusion), channel_id=1, source_target_pairs={{0,8},{1,9},{2,10},{3,11},{4,12},{5,13},{6,14},{7,15},{8,0},{9,1},... | collective-permute-start | bytes 3145736 | tf_op jit(solution)/shard_map/ppermute | solution.py:50
  262.3 56.2 %collective-permute-start.43 = (bf16[1728,256]{1,0:T(8,128)(2,1)}, bf16[1728,256]{1,0:T(8,128)(2,1)}, u32[]{:S(2)}, u32[]{:S(2)}) collective-permute-start(bf16[1728,256]{1,0:T(8,128)(2,1)} %convert_add_fusion.4), channel_id=1, source_target_pairs={{2,0},{3,1},{0,2},{1,3},{6,4},{7,5},{4,6},{5,7},{10,8},{11,9},{8,1... | collective-permute-start | bytes 2654216 | tf_op jit(solution)/shard_map/ppermute | solution.py:50
  264.1 27.9 %collective-permute-start.42 = (bf16[1728,256]{1,0:T(8,128)(2,1)}, bf16[1728,256]{1,0:T(8,128)(2,1)}, u32[]{:S(2)}, u32[]{:S(2)}) collective-permute-start(bf16[1728,256]{1,0:T(8,128)(2,1)} %get-tuple-element.98), channel_id=1, source_target_pairs={{0,16},{1,17},{2,18},{3,19},{4,20},{5,21},{6,22},{7,23},{8,24},{9,... | collective-permute-start | bytes 2654216 | tf_op jit(solution)/shard_map/ppermute | solution.py:50
  286.5 32.0 %collective-permute-start.41 = (bf16[512,2048]{1,0:T(8,128)(2,1)S(1)}, bf16[512,2048]{1,0:T(8,128)(2,1)S(1)}, u32[]{:S(2)}, u32[]{:S(2)}) collective-permute-start(bf16[512,2048]{1,0:T(8,128)(2,1)S(1)} %pad_maximum_fusion.8), channel_id=1, source_target_pairs={{0,4},{1,5},{2,6},{3,7},{4,0},{5,1},{6,2},{7,3},{8,12},{9,13},{10,... | collective-permute-start | bytes 6291464 | tf_op jit(solution)/shard_map/ppermute | solution.py:50
  290.1 24.8 %collective-permute-start.39 = (bf16[512,1024]{1,0:T(8,128)(2,1)}, bf16[512,1024]{1,0:T(8,128)(2,1)}, u32[]{:S(2)}, u32[]{:S(2)}) collective-permute-start(bf16[512,1024]{1,0:T(8,128)(2,1)} %slice_dynamic-update-slice_fusion.8), channel_id=1, source_target_pairs={{0,8},{1,9},{2,10},{3,11},{4,12},{5,13},{6,14},{7,15},{8,0},{9,1},... | collective-permute-start | bytes 3145736 | tf_op jit(solution)/shard_map/ppermute | solution.py:50
  321.1 47.3 %collective-permute-start.44 = (bf16[512,2048]{1,0:T(8,128)(2,1)}, bf16[512,2048]{1,0:T(8,128)(2,1)}, u32[]{:S(2)}, u32[]{:S(2)}) collective-permute-start(bf16[512,2048]{1,0:T(8,128)(2,1)} %convolution_convert_fusion.1), channel_id=1, source_target_pairs={{0,4},{1,5},{2,6},{3,7},{4,0},{5,1},{6,2},{7,3},{8,12},{9,13},{10,... | collective-permute-start | bytes 6291464 | tf_op jit(solution)/shard_map/ppermute | solution.py:50
  363.2 28.5 %collective-permute-start.52 = (bf16[128,512]{1,0:T(8,128)(2,1)S(1)}, bf16[128,512]{1,0:T(8,128)(2,1)S(1)}, u32[]{:S(2)}, u32[]{:S(2)}) collective-permute-start(bf16[128,512]{1,0:T(8,128)(2,1)S(1)} %pad_maximum_fusion.22), channel_id=1, source_target_pairs={{3,0},{0,1},{1,2},{2,3},{7,4},{4,5},{5,6},{6,7},{11,8},{8,9},{9,10... | collective-permute-start | bytes 393224 | tf_op jit(solution)/shard_map/ppermute | solution.py:50
  364.2 27.5 %collective-permute-start.53 = (bf16[128,512]{1,0:T(8,128)(2,1)S(1)}, bf16[128,512]{1,0:T(8,128)(2,1)S(1)}, u32[]{:S(2)}, u32[]{:S(2)}) collective-permute-start(bf16[128,512]{1,0:T(8,128)(2,1)S(1)} %pad_maximum_fusion.23), channel_id=1, source_target_pairs={{2,0},{3,1},{0,2},{1,3},{6,4},{7,5},{4,6},{5,7},{10,8},{11,9},{8,1... | collective-permute-start | bytes 393224 | tf_op jit(solution)/shard_map/ppermute | solution.py:50
  366.6 25.1 %collective-permute-start.54 = (bf16[128,512]{1,0:T(8,128)(2,1)S(1)}, bf16[128,512]{1,0:T(8,128)(2,1)S(1)}, u32[]{:S(2)}, u32[]{:S(2)}) collective-permute-start(bf16[128,512]{1,0:T(8,128)(2,1)S(1)} %pad_maximum_fusion.24), channel_id=1, source_target_pairs={{1,0},{2,1},{3,2},{0,3},{5,4},{6,5},{7,6},{4,7},{9,8},{10,9},{11,1... | collective-permute-start | bytes 393224 | tf_op jit(solution)/shard_map/ppermute | solution.py:50
  (102 other events, 1094.7 us)
